TPU v7x, 512 devices: a whole 4x4x16 slice. The times are simulated.
512 devices in a mesh: grp: 64 (over z, y), seq: 8 (over x, core).
Axes of the slice: x: 4, y: 4, z: 16, core: 2. Of those that a mesh axis runs over, the one named last changes fastest.
Arguments:
- tokens: bfloat16 [64, 1024, 2048], P('grp', 'seq'), may hold values from -6 to 6
- seg_ids: int32 [64, 1024], P('grp'), may hold values from 0 to 3, never falling along the last dimension, each value on 1 to 512 neighbouring positions
- deal: int32 [64, 1024], P('grp'), may hold values from 0 to 1023, each once within a row
- page_table: int32 [64, 128], P('grp'), may hold values from 0 to 127, each once within a row
- in_gain: float32 [2048], replicated, may hold values from 0.1 to 1.9
- w_query: bfloat16 [2048, 2048], P('grp', 'seq'), may hold values from -0.125 to 0.125
- key_projection_weight: bfloat16 [2048, 512], P('grp'), may hold values from -0.125 to 0.125
- value_projection_weight: bfloat16 [2048, 512], P('grp'), may hold values from -0.125 to 0.125
- q_gain: float32 [256], replicated, may hold values from 1.25 to 3.75
- key_norm_gain: float32 [256], replicated, may hold values from 0.1 to 1.9
- w_out: bfloat16 [2048, 2048], P('seq', 'grp'), may hold values from -0.125 to 0.125
- post_gain: float32 [2048], replicated, may hold values from 0.1 to 1.9
- final_gain: float32 [2048], replicated, may hold values from 0.1 to 1.9
- embed: bfloat16 [262144, 2048], P(('grp', 'seq')), may hold values from -0.375 to 0.375
Outputs:
- hidden_out: bfloat16 [64, 1024, 2048], P('grp', 'seq')
- kv_cache: bfloat16 [64, 128, 8, 1024], P('grp', 'seq')
- last_norm: float32 [256], replicated
- max_logit: float32 [256], replicated
Inputs may be any that keep to these rules, and one draw needn't show every extreme that they name: `seg_ids`: along each pack the prompt numbers never fall; every one of the 4 prompts occurs, none has more than 512 positions, and one has exactly that many. Each row of deal holds every packed position once. Each row of page_table holds every page of the pack once.
All inputs are finite; a program needn't handle non-finite values.
Results may differ from a plain program's by a relative error of at most 0.015.
The roundings to bfloat16 on the way count: a program that leaves them out, or rounds other values in their place, can miss the bound.
Values may be sent and summed in bfloat16 or wider, within the bound.
A program may use at most 64 MiB of HBM per device.

v0:
```python
import jax
import jax.numpy as jnp
from jax import lax
from jax.sharding import PartitionSpec as P

QUERY_HEADS = 8
KEY_HEADS = 2
PAGE_SLOTS = 8
SEGS = 4


eps = 1e-06
rope_base = 1000000.0
cap_value = 30.0


def rows_scaled(value_rows, scales):
    mean_square = jnp.mean(value_rows * value_rows, axis=-1, keepdims=True)
    return value_rows * lax.rsqrt(mean_square + eps) * scales


def rotate(value_rows, offsets):
    half_width = value_rows.shape[-1] // 2
    frequency = rope_base ** (
        -2.0 * jnp.arange(half_width, dtype=jnp.float32) / value_rows.shape[-1]
    )
    angles = offsets.astype(jnp.float32)[:, None] * frequency[None, :]
    cosine = jnp.cos(angles)[:, None, :]
    sine_table = jnp.sin(angles)[:, None, :]
    lower_half = value_rows[..., :half_width]
    upper_half = value_rows[..., half_width:]
    return jnp.concatenate(
        [
            lower_half * cosine - upper_half * sine_table,
            upper_half * cosine + lower_half * sine_table,
        ],
        axis=-1,
    )


def layout(segment, dealing):
    row_seg = jnp.take(segment, dealing)
    before = jnp.sum((segment[None, :] < row_seg[:, None]).astype(jnp.int32), axis=1)
    return (row_seg, dealing - before)


def attend(query, key_selected, value_selected, row_seg, dealing):
    scores = jnp.einsum("qhd,khd->hqk", query, key_selected, preferred_element_type=jnp.float32)
    allowed = (row_seg[:, None] == row_seg[None, :]) & (dealing[None, :] <= dealing[:, None])
    masked = jnp.where(allowed[None], scores, -1e30)
    row_peak = jnp.max(masked, axis=-1, keepdims=True)
    raw_weights = jnp.where(allowed[None], jnp.exp(masked - row_peak), 0.0)
    row_total = jnp.sum(raw_weights, axis=-1, keepdims=True)
    weights = (raw_weights / row_total).astype(jnp.bfloat16)
    attended = jnp.einsum(
        "hqk,khd->qhd", weights, value_selected, preferred_element_type=jnp.float32
    )
    return attended.astype(jnp.bfloat16).reshape(query.shape[0], -1)


def shards(
    tokens,
    seg_ids,
    deal,
    page_table,
    in_gain,
    w_query,
    key_projection_weight,
    value_projection_weight,
    q_gain,
    key_norm_gain,
    w_out,
    post_gain,
    final_gain,
    embed,
):
    own_tokens = tokens[0]
    rows_dev = own_tokens.shape[0]
    segment = seg_ids[0]
    dealing = deal[0]
    width_of_head = q_gain.shape[0]
    heads_local = w_query.shape[1] // width_of_head
    sequence_index = lax.axis_index("seq")
    own_start = sequence_index * rows_dev
    row_seg, offsets = layout(segment, dealing)
    normed_own = rows_scaled(own_tokens.astype(jnp.float32), in_gain).astype(jnp.bfloat16)
    normed_all = lax.all_gather(normed_own, "seq", axis=0, tiled=True)
    rows_of_pack = normed_all.shape[0]
    key_value_offsets = lax.dynamic_slice_in_dim(offsets, own_start, rows_dev, 0)
    query_full, key_full, value_full, out_full = (
        lax.all_gather(w_query, "grp", axis=0, tiled=True),
        lax.all_gather(key_projection_weight, "grp", axis=0, tiled=True),
        lax.all_gather(value_projection_weight, "grp", axis=0, tiled=True),
        lax.all_gather(w_out, "grp", axis=1, tiled=True),
    )
    query_raw = jnp.dot(normed_all, query_full, preferred_element_type=jnp.float32)
    key_unnormed = jnp.dot(normed_own, key_full, preferred_element_type=jnp.float32)
    value_unnormed = jnp.dot(normed_own, value_full, preferred_element_type=jnp.float32)
    query = rotate(
        rows_scaled(query_raw.reshape(rows_of_pack, heads_local, width_of_head), q_gain), offsets
    ).astype(jnp.bfloat16)
    rows_of_source = normed_own.shape[0]
    key_local_part = rotate(
        rows_scaled(key_unnormed.reshape(rows_of_source, KEY_HEADS, width_of_head), key_norm_gain),
        key_value_offsets,
    ).astype(jnp.bfloat16)
    value_local_part = rows_scaled(
        value_unnormed.reshape(rows_of_source, KEY_HEADS, width_of_head), 1.0
    ).astype(jnp.bfloat16)
    key_local_part = key_local_part.reshape(rows_of_source, KEY_HEADS * width_of_head)
    value_local_part = value_local_part.reshape(rows_of_source, KEY_HEADS * width_of_head)
    key_gathered, value_gathered = (
        lax.all_gather(key_local_part, "seq", axis=0, tiled=True),
        lax.all_gather(value_local_part, "seq", axis=0, tiled=True),
    )
    index_of_head = (sequence_index * heads_local + jnp.arange(heads_local, dtype=jnp.int32)) // (
        QUERY_HEADS // KEY_HEADS
    )
    key_selected = jnp.take(
        key_gathered.reshape(rows_of_pack, KEY_HEADS, width_of_head), index_of_head, axis=1
    )
    value_selected = jnp.take(
        value_gathered.reshape(rows_of_pack, KEY_HEADS, width_of_head), index_of_head, axis=1
    )
    attended = attend(query, key_selected, value_selected, row_seg, dealing)
    partial_out = jnp.dot(attended, out_full, preferred_element_type=jnp.float32)
    summed = lax.psum_scatter(
        partial_out.astype(jnp.bfloat16), "seq", scatter_dimension=0, tiled=True
    ).astype(jnp.float32)
    hidden = (own_tokens.astype(jnp.float32) + rows_scaled(summed, post_gain)).astype(jnp.bfloat16)
    inverse_assignment = jnp.argsort(dealing)
    inverse_page = jnp.argsort(page_table[0])
    own_pages = rows_dev // PAGE_SLOTS
    physical = sequence_index * own_pages + jnp.arange(own_pages, dtype=jnp.int32)
    logical_index = jnp.take(inverse_page, physical)
    packed = logical_index[:, None] * PAGE_SLOTS + jnp.arange(PAGE_SLOTS, dtype=jnp.int32)[None, :]
    source_index = jnp.take(inverse_assignment, packed.reshape(-1))
    stacked_rows = jnp.concatenate([key_gathered, value_gathered], axis=1)
    cache_pages = jnp.take(stacked_rows, source_index, axis=0).reshape(
        own_pages, PAGE_SLOTS, stacked_rows.shape[1]
    )
    last_pos = (
        jnp.sum(
            (segment[None, :] <= jnp.arange(SEGS, dtype=jnp.int32)[:, None]).astype(jnp.int32),
            axis=1,
        )
        - 1
    )
    local_row = jnp.take(inverse_assignment, last_pos) - own_start
    selector = (local_row[:, None] == jnp.arange(rows_dev, dtype=jnp.int32)[None, :]).astype(
        jnp.bfloat16
    )
    group_states = jnp.dot(selector, hidden, preferred_element_type=jnp.float32)
    pack_states = lax.psum(group_states.astype(jnp.bfloat16), "seq")
    states = lax.all_gather(pack_states, "grp", axis=0, tiled=True).astype(jnp.float32)
    last_norm = jnp.sqrt(jnp.mean(states * states, axis=-1))
    final = rows_scaled(states, final_gain).astype(jnp.bfloat16)
    logits = lax.dot_general(
        final, embed, (((1,), (1,)), ((), ())), preferred_element_type=jnp.float32
    )
    shard_max = jnp.max(cap_value * jnp.tanh(logits / cap_value), axis=1)
    max_logit = lax.pmax(shard_max, ("grp", "seq"))
    return (hidden[None], cache_pages[None], last_norm, max_logit)


def solution(mesh):
    return jax.shard_map(
        shards,
        mesh=mesh,
        in_specs=(
            P("grp", "seq", None),
            P("grp", None),
            P("grp", None),
            P("grp", None),
            P(),
            P("grp", "seq"),
            P("grp", None),
            P("grp", None),
            P(),
            P(),
            P("seq", "grp"),
            P(),
            P(),
            P(("grp", "seq"), None),
        ),
        out_specs=(P("grp", "seq", None), P("grp", "seq", None, None), P(), P()),
        check_vma=False,
    )
```

profile of v0, /device:TPU:1, one launch (start us, length us, event | category | flops | bytes accessed | tf_op | source)
XLA Modules:
  0.0 1011.3 jit_solution(3232940448721086610)
XLA Ops:
  9.5 5.7 gather_fusion
  16.3 132.1 %all-gather.18.cloned.1.call-done = bf16[2048,512]{1,0:T(8,128)(2,1)} async-done(((bf16[32,512]{1,0:T(8,128)(2,1)}), bf16[2048,512]{1,0:T(8,128)(2,1)}) %all-gather.18.cloned.1.call-update) | async-done | bytes 2097168 | tf_op jit(solution)/shard_map/all_gather | solution.py:92
  148.5 3.9 copy.40
  152.4 2.5 multiply_reduce_fusion.2
  156.1 132.3 %all-gather.10.cloned.1.call-done = bf16[2048,512]{1,0:T(8,128)(2,1)} async-done(((bf16[32,512]{1,0:T(8,128)(2,1)}), bf16[2048,512]{1,0:T(8,128)(2,1)}) %all-gather.10.cloned.1.call-update) | async-done | bytes 2097168 | tf_op jit(solution)/shard_map/all_gather | solution.py:93
  288.4 4.0 copy.36
  292.4 2.5 multiply_reduce_fusion.3
  298.6 29.0 %all-gather.20.cloned.1.call-done = bf16[1024,512]{1,0:T(8,128)(2,1)} async-done(((bf16[128,512]{1,0:T(8,128)(2,1)}), bf16[1024,512]{1,0:T(8,128)(2,1)}) %all-gather.20.cloned.1.call-update) | async-done | bytes 1048592 | tf_op jit(solution)/shard_map/all_gather | solution.py:113
  327.6 2.2 reshape.529
  329.8 3.3 constant_dynamic-slice_fusion
  333.1 27.5 %all-gather.12.cloned.1.call-done = bf16[1024,512]{1,0:T(8,128)(2,1)} async-done(((bf16[128,512]{1,0:T(8,128)(2,1)}), bf16[1024,512]{1,0:T(8,128)(2,1)}) %all-gather.12.cloned.1.call-update) | async-done | bytes 1048592 | tf_op jit(solution)/shard_map/all_gather | solution.py:114
  360.6 2.2 reshape.527
  362.8 3.3 constant_dynamic-slice_fusion.1
  366.1 126.2 %all-gather.16.cloned.1.call-done = bf16[2048,256]{1,0:T(8,128)(2,1)} async-done(((bf16[32,256]{1,0:T(8,128)(2,1)}), bf16[2048,256]{1,0:T(8,128)(2,1)}) %all-gather.16.cloned.1.call-update) | async-done | bytes 1048592 | tf_op jit(solution)/shard_map/all_gather | solution.py:91
  492.3 48.3 %all-gather.14.cloned.1.call-done = bf16[1024,2048]{1,0:T(8,128)(2,1)} async-done(((bf16[128,2048]{1,0:T(8,128)(2,1)}), bf16[1024,2048]{1,0:T(8,128)(2,1)}) %all-gather.14.cloned.1.call-update) | async-done | bytes 4194320 | tf_op jit(solution)/shard_map/all_gather | solution.py:87
  540.6 3.9 multiply_reduce_fusion.1
  544.7 2.3 fusion.46
  548.0 2.0 copy-done.3
  551.5 121.2 %all-gather.22.cloned.1.call-done = bf16[256,2048]{0,1:T(8,128)(2,1)} async-done(((bf16[256,32]{0,1:T(8,128)(2,1)}), bf16[256,2048]{0,1:T(8,128)(2,1)}) %all-gather.22.cloned.1.call-update) | async-done | bytes 1048592 | tf_op jit(solution)/shard_map/all_gather | solution.py:94
  672.7 7.6 convolution_convert_fusion
  680.4 4.4 sort.35
  684.8 2.5 sort.34
  688.8 40.6 %reduce-scatter.2.cloned.1.call-done = bf16[128,2048]{1,0:T(8,128)(2,1)} async-done(((bf16[1024,2048]{1,0:T(8,128)(2,1)}), bf16[128,2048]{1,0:T(8,128)(2,1)}) %reduce-scatter.2.cloned.1.call-update) | async-done | bytes 524304 | tf_op jit(solution)/shard_map/reduce_scatter | solution.py:127
  730.6 1.5 convolution_convert_fusion.1
  732.1 24.1 %psum.7 = bf16[4,2048]{1,0:T(4,128)(2,1)} all-reduce(bf16[4,2048]{1,0:T(4,128)(2,1)S(1)} %convolution_convert_fusion.1), channel_id=1, replica_groups=mesh['grp'=64,'seq'=8] {'seq'}, use_global_device_ids=true, to_apply=%region_12.14 | all-reduce | flops 8192 | bytes 32768 | tf_op jit(solution)/shard_map/psum | solution.py:154
  757.6 3.2 pad_maximum_fusion
  760.8 2.9 gather_fusion.3
  765.5 121.9 %all-gather.24.cloned.1.call-done = bf16[64,4,2048]{2,1,0:T(4,128)(2,1)} async-done(((bf16[1,4,2048]{2,1,0:T(4,128)(2,1)}), bf16[64,4,2048]{2,1,0:T(4,128)(2,1)}) %all-gather.24.cloned.1.call-update) | async-done | bytes 1048592 | tf_op jit(solution)/shard_map/all_gather | solution.py:155
  887.5 2.5 reshape.630
  890.0 1.8 multiply_reduce_fusion
  892.3 2.4 fusion.10
  894.8 110.0 %pmax.7 = f32[256]{0:T(256)} all-reduce(f32[256]{0:T(256)S(1)} %fusion.10), channel_id=1, replica_groups=mesh['grp'=64,'seq'=8] {'grp','seq'}, use_global_device_ids=true, to_apply=%region_15.17 | all-reduce | flops 256 | bytes 2048 | tf_op jit(solution)/shard_map/pmax | solution.py:162
  (94 shorter events, 17.3 us)
Async XLA Ops:
  7.2 885.2 %copy-start = (bf16[512,2048]{1,0:T(8,128)(2,1)S(1)}, bf16[512,2048]{1,0:T(8,128)(2,1)}, u32[]{:S(2)}) copy-start(bf16[512,2048]{1,0:T(8,128)(2,1)} %param.29) | copy-start | bytes 6291460
  7.2 8.0 copy-start.6
  7.2 8.1 copy-start.1
  7.2 8.6 copy-start.2
  7.2 141.2 %all-gather.18.cloned.1.call-start = ((), (), s32[]{:S(2)}) async-start(), calls=%async_computation.5 | async-start | bytes 2129920 | tf_op jit(solution)/shard_map/all_gather | solution.py:92
  7.9 280.5 %all-gather.10.cloned.1.call-start = ((), (), s32[]{:S(2)}) async-start(), calls=%async_computation.1 | async-start | bytes 2129920 | tf_op jit(solution)/shard_map/all_gather | solution.py:93
  8.7 318.9 %all-gather.20.cloned.1.call-start = ((), (), s32[]{:S(2)}) async-start(), calls=%async_computation.6 | async-start | bytes 1179648 | tf_op jit(solution)/shard_map/all_gather | solution.py:113
  9.4 143.0 %copy-start.7 = (f32[2048]{0:T(1024)S(1)}, f32[2048]{0:T(1024)}, u32[]{:S(2)}) copy-start(f32[2048]{0:T(1024)} %param.20) | copy-start | bytes 24580
  15.2 139.7 %copy-start.9 = (f32[256]{0:T(256)S(1)}, f32[256]{0:T(256)}, u32[]{:S(2)}) copy-start(f32[256]{0:T(256)} %param.25) | copy-start | bytes 3076
  156.0 204.6 %all-gather.12.cloned.1.call-start = ((), (), s32[]{:S(2)}) async-start(), calls=%async_computation.2 | async-start | bytes 1179648 | tf_op jit(solution)/shard_map/all_gather | solution.py:114
  295.9 196.3 %all-gather.16.cloned.1.call-start = ((), (), s32[]{:S(2)}) async-start(), calls=%async_computation.4 | async-start | bytes 1064960 | tf_op jit(solution)/shard_map/all_gather | solution.py:91
  296.5 244.1 %all-gather.14.cloned.1.call-start = ((), (), s32[]{:S(2)}) async-start(), calls=%async_computation.3 | async-start | bytes 4718592 | tf_op jit(solution)/shard_map/all_gather | solution.py:87
  297.6 375.1 %all-gather.22.cloned.1.call-start = ((), (), s32[]{:S(2)}) async-start(), calls=%async_computation.7 | async-start | bytes 1064960 | tf_op jit(solution)/shard_map/all_gather | solution.py:94
  298.3 431.1 %reduce-scatter.2.cloned.1.call-start = ((), (), s32[]{:S(2)}) async-start(), calls=%async_computation.8 | async-start | bytes 4718592 | tf_op jit(solution)/shard_map/reduce_scatter | solution.py:127
  366.1 178.5 %copy-start.10 = (f32[256]{0:T(256)S(1)}, f32[256]{0:T(256)}, u32[]{:S(2)}) copy-start(f32[256]{0:T(256)} %param.24) | copy-start | bytes 3076
  540.6 6.4 copy-start.5
  548.0 2.0 copy-start.3
  680.3 4.5 copy-start.12
  680.3 50.3 %copy-start.8 = (f32[2048]{0:T(1024)S(1)}, f32[2048]{0:T(1024)}, u32[]{:S(2)}) copy-start(f32[2048]{0:T(1024)} %param.27) | copy-start | bytes 24580
  680.3 207.2 %all-gather.24.cloned.1.call-start = ((), (), s32[]{:S(2)}) async-start(), calls=%async_computation.9 | async-start | bytes 1064960 | tf_op jit(solution)/shard_map/all_gather | solution.py:155
  730.6 33.9 %copy-start.4 = (bf16[128,2048]{1,0:T(8,128)(2,1)S(1)}, bf16[128,2048]{1,0:T(8,128)(2,1)}, u32[]{:S(2)}) copy-start(bf16[128,2048]{1,0:T(8,128)(2,1)} %reduce-scatter.2.cloned.1.call-done) | copy-start | bytes 1572868
  763.7 128.7 %copy-start.11 = (f32[2048]{0:T(1024)S(1)}, f32[2048]{0:T(1024)}, u32[]{:S(2)}) copy-start(f32[2048]{0:T(1024)} %param.28) | copy-start | bytes 24580
Sparse Core Ops, SparseCore 0:
  11.0 137.4 all-gather.17
  151.4 136.9 all-gather.9
  291.1 36.4 all-gather.19
  329.6 30.9 all-gather.11
  363.4 128.8 all-gather.15
  494.8 45.7 all-gather.13
  543.6 129.0 all-gather.21
  680.5 48.8 reduce-scatter.1
  756.3 131.0 all-gather.23
where the time goes:
time: 1010 us
  waiting for transfers between devices  782 us (77%)
  blocking collectives  134 us (13%)
  local copies, waits for them, and re-layouts  36.2 us (4%)
  other arithmetic  22.9 us (2%)
  matrix products  21.4 us (2%)
  between operations  14.2 us (1%)
    all_gather x1, waiting for transfers between devices, shards(): lax.all_gather(value_projection_weight, 'grp', axis=0, tiled=True)  132 us
    all_gather x1, waiting for transfers between devices, shards(): lax.all_gather(key_projection_weight, 'grp', axis=0, tiled=True)  132 us
    all_gather x1, waiting for transfers between devices, shards(): lax.all_gather(w_query, 'grp', axis=0, tiled=True)  126 us
    all_gather x1, waiting for transfers between devices, shards(): lax.all_gather(pack_states, 'grp', axis=0, tiled=True).astype(jnp.float32)  122 us
    all_gather x1, waiting for transfers between devices, shards(): lax.all_gather(w_out, 'grp', axis=1, tiled=True)  121 us
    pmax x1, blocking collectives, shards(): max_logit = lax.pmax(shard_max, ('grp', 'seq'))  110 us
    all_gather x1, waiting for transfers between devices, shards(): normed_all = lax.all_gather(normed_own, 'seq', axis=0, tiled=True)  48.3 us
    reduce_scatter x1, waiting for transfers between devices, shards(): lax.psum_scatter(partial_out.astype(jnp.bfloat16), 'seq', scatter_dimensi...  40.6 us
  transfers between devices with their start and end apart: 9, of which 9 were waited for; matrix products, arithmetic and copies ran while one was open for 6% of the time, Pallas kernels for 0%

commit v1 on v0

v1 whole, which is shorter than its diff:
```python
import functools

import jax
import jax.numpy as jnp
from jax import lax
from jax.experimental import pallas as pl
from jax.experimental.pallas import tpu as pltpu
from jax.sharding import PartitionSpec as P

MESH = pl.DeviceIdType.MESH
ANY = pl.BlockSpec(memory_space=pl.ANY)
VMEM = pl.BlockSpec(memory_space=pltpu.VMEM)
BF16 = jnp.bfloat16
F32 = jnp.float32
DMA = pltpu.SemaphoreType.DMA

KEY_HEADS = 2
SEGS = 4
NY = 4
NX = 4
NS = 8
CHUNKS = 4
eps = 1e-06
rope_base = 1000000.0
cap_value = 30.0


def remote(src, dst, send_sem, recv_sem, device):
    return pltpu.make_async_remote_copy(
        src_ref=src,
        dst_ref=dst,
        send_sem=send_sem,
        recv_sem=recv_sem,
        device_id=device,
        device_id_type=MESH,
    )


class Place:
    def __init__(self, nz):
        self.nz = nz
        self.g = lax.axis_index("grp")
        self.s = lax.axis_index("seq")
        self.z, self.y = self.g // NY, self.g % NY
        self.x, self.c = self.s // 2, self.s % 2
        self.sib = {"seq": 2 * self.x + 1 - self.c}

    def zn(self, d):
        return {"grp": ((self.z + d + self.nz) % self.nz) * NY + self.y}

    def yn(self, d):
        return {"grp": self.z * NY + (self.y + d + NY) % NY}

    def xs(self, d):
        return 2 * ((self.x + d + NX) % NX) + self.c

    def xn(self, d):
        return {"seq": self.xs(d)}

    def sn(self, d):
        return {"seq": (self.s + d) % NS}


class Link:
    def __init__(self, place):
        self.place = place
        self.sent = []

    def send(self, src, dst, send_sem, recv_sem, device):
        copy = remote(src, dst, send_sem, recv_sem, device)
        copy.start()
        self.sent.append(copy)

    def arrived(self, dst, send_sem, recv_sem):
        remote(dst, dst, send_sem, recv_sem, self.place.sib).wait_recv()

    def finish(self):
        for copy in self.sent:
            copy.wait_send()


def barrier(devices):
    sem = pltpu.get_barrier_semaphore()
    for device in devices:
        pl.semaphore_signal(sem, inc=1, device_id=device, device_id_type=MESH)
    pl.semaphore_wait(sem, len(devices))


def slots(place, k):
    nz = place.nz
    half = nz // 2
    if k == 0:
        return [(0, place.z, 1)]
    if k > half:
        return []
    up = (k, (place.z - k + nz) % nz, 1)
    if k == half:
        return [up]
    return [up, (half + k, (place.z + k) % nz, -1)]


def gather_rows(place, link, own, every, ss, rs):
    step = own.shape[0] // CHUNKS
    piece = lambda s, j: every.at[s, pl.ds(j * step, step)]
    s, left, right, far = place.s, place.xs(-1), place.xs(1), place.xs(2)
    for j in range(CHUNKS):
        mine = own.at[pl.ds(j * step, step)]
        link.send(mine, piece(s, j), ss.at[0, j], rs.at[s, j], place.xn(1))
        link.send(mine, piece(s, j), ss.at[1, j], rs.at[s, j], place.xn(-1))
        link.send(mine, piece(s, j), ss.at[2, j], rs.at[s, j], place.sib)
    keep = pltpu.make_async_copy(own, every.at[s], ss.at[7, 0])
    keep.start()
    yield
    for j in range(CHUNKS):
        link.arrived(piece(left, j), ss.at[0, 0], rs.at[left, j])
        if 2 * j < CHUNKS:
            link.send(piece(left, j), piece(left, j), ss.at[3, j], rs.at[left, j], place.xn(1))
        link.send(piece(left, j), piece(left, j), ss.at[4, j], rs.at[left, j], place.sib)
        link.arrived(piece(right, j), ss.at[0, 0], rs.at[right, j])
        if 2 * j >= CHUNKS:
            link.send(piece(right, j), piece(right, j), ss.at[3, j], rs.at[right, j], place.xn(-1))
        link.send(piece(right, j), piece(right, j), ss.at[5, j], rs.at[right, j], place.sib)
        yield
    for j in range(CHUNKS):
        link.arrived(piece(far, j), ss.at[0, 0], rs.at[far, j])
        link.send(piece(far, j), piece(far, j), ss.at[6, j], rs.at[far, j], place.sib)
        yield
    for x in range(NX):
        other = 2 * x + 1 - place.c
        for j in range(CHUNKS):
            link.arrived(piece(other, j), ss.at[0, 0], rs.at[other, j])
    keep.wait()


def gather_zy(place, link, block, plane, other_plane, sems):
    zs, zr, ys, yr, ss, sr = sems
    half = place.nz // 2
    gy = lambda z, d: z * NY + (place.y + d + NY) % NY
    for k in range(half + 3):
        for q, z, way in slots(place, k):
            here = block(gy(z, 0))
            if k > 0:
                link.arrived(here, zs.at[q], zr.at[q])
            if k == 0:
                link.send(here, here, zs.at[1], zr.at[1], place.zn(1))
                if half > 1:
                    link.send(here, here, zs.at[half + 1], zr.at[half + 1], place.zn(-1))
            elif way == 1 and k < half:
                link.send(here, here, zs.at[q + 1], zr.at[q + 1], place.zn(1))
            elif way == -1 and k < half - 1:
                link.send(here, here, zs.at[q + 1], zr.at[q + 1], place.zn(-1))
            link.send(here, here, ys.at[0, q], yr.at[0, q], place.yn(1))
            link.send(here, here, ys.at[1, q], yr.at[1, q], place.yn(-1))
        for q, z, way in slots(place, k - 1) if k >= 1 else []:
            near = block(gy(z, -way))
            kind = 0 if way == 1 else 1
            link.arrived(near, zs.at[0], yr.at[kind, q])
            link.send(near, near, ys.at[2, q], yr.at[2, q], place.yn(way))
        for q, z, way in slots(place, k - 2) if k >= 2 else []:
            link.arrived(block(gy(z, way)), zs.at[0], yr.at[1 if way == 1 else 0, q])
            link.arrived(block(gy(z, 2)), zs.at[0], yr.at[2, q])
            link.send(plane(z), plane(z), ss.at[q], sr.at[q], place.sib)
        yield
    for k in range(half + 1):
        for q, z, way in slots(place, k):
            link.arrived(other_plane(z), zs.at[0], sr.at[q])


def gather_yz(place, link, block, plane, other_plane, sems):
    zs, zr, ys, yr, ss, sr = sems
    half = place.nz // 2
    gy = lambda d: place.z * NY + (place.y + d + NY) % NY
    here = block(gy(0))
    link.send(here, here, ys.at[0], yr.at[0], place.yn(1))
    link.send(here, here, ys.at[1], yr.at[1], place.yn(-1))
    yield
    near = block(gy(-1))
    link.arrived(near, zs.at[0], yr.at[0])
    link.send(near, near, ys.at[2], yr.at[2], place.yn(1))
    link.arrived(block(gy(1)), zs.at[0], yr.at[1])
    link.arrived(block(gy(2)), zs.at[0], yr.at[2])
    for k in range(half + 1):
        for q, z, way in slots(place, k):
            here = plane(z)
            if k > 0:
                link.arrived(here, zs.at[q], zr.at[q])
            if k == 0:
                link.send(here, here, zs.at[1], zr.at[1], place.zn(1))
                if half > 1:
                    link.send(here, here, zs.at[half + 1], zr.at[half + 1], place.zn(-1))
            elif way == 1 and k < half:
                link.send(here, here, zs.at[q + 1], zr.at[q + 1], place.zn(1))
            elif way == -1 and k < half - 1:
                link.send(here, here, zs.at[q + 1], zr.at[q + 1], place.zn(-1))
            link.send(here, here, ss.at[q], sr.at[q], place.sib)
        yield
    for k in range(half + 1):
        for q, z, way in slots(place, k):
            link.arrived(other_plane(z), zs.at[0], sr.at[q])


def gather_out(place, link, wo_all, xs, xr, first, second):
    g, c = place.g, place.c
    own = wo_all.at[place.x, c, g]
    for n, d in enumerate((1, -1, 2)):
        link.send(own, own, xs.at[n], xr.at[n], place.xn(d))
    yield
    for n, d in enumerate((1, -1, 2)):
        link.arrived(wo_all.at[(place.x - d + NX) % NX, c, g], xs.at[0], xr.at[n])
    half = NX // 2
    low = lambda g: wo_all.at[pl.ds(0, half), c, g]
    high = lambda g: wo_all.at[pl.ds(half, half), c, g]
    low_plane = lambda c: lambda z: wo_all.at[pl.ds(0, half), c, pl.ds(z * NY, NY)]
    high_plane = lambda c: lambda z: wo_all.at[pl.ds(half, half), c, pl.ds(z * NY, NY)]
    gens = [
        gather_zy(place, link, low, low_plane(c), low_plane(1 - c), first),
        gather_yz(place, link, high, high_plane(c), high_plane(1 - c), second),
    ]
    yield from together(gens)


def together(gens):
    gens = list(gens)
    while gens:
        for gen in list(gens):
            if next(gen, "end") == "end":
                gens.remove(gen)
        yield


def gather_kernel(nz, tok, w, wo, tok_all, w_all, wo_all, ls, ts, tr, *sems):
    place = Place(nz)
    link = Link(place)
    g, c = place.g, place.c
    width = w.shape[1] // 2
    lanes = lambda start, size: pl.ds(pl.multiple_of(start, 128), size)
    keep = [
        pltpu.make_async_copy(w, w_all.at[g, :, lanes(c * width, 2 * width)], ls.at[0]),
        pltpu.make_async_copy(wo, wo_all.at[place.x, c, g], ls.at[1]),
    ]
    for copy in keep:
        copy.start()
    barrier(
        [place.zn(1), place.zn(-1), place.yn(1), place.yn(-1)]
        + [place.xn(1), place.xn(-1), place.xn(2), place.sib]
    )
    for copy in keep:
        copy.wait()
    block = lambda g: w_all.at[g, :, lanes(c * width, 2 * width)]
    plane = lambda z: w_all.at[pl.ds(z * NY, NY), :, lanes(c * 2 * width, width)]
    other = lambda z: w_all.at[pl.ds(z * NY, NY), :, lanes((1 - c) * 2 * width, width)]
    gens = [
        gather_zy(place, link, block, plane, other, sems[0:6]),
        gather_rows(place, link, tok, tok_all, ts, tr),
        gather_out(place, link, wo_all, sems[6], sems[7], sems[8:14], sems[14:20]),
    ]
    for _ in together(gens):
        pass
    link.finish()


def gather_call(nz, tok, w, wo):
    rows, model = tok.shape
    depth, width = w.shape[0], w.shape[1] // 2
    grp = nz * NY
    ring = [DMA((nz,)), DMA((nz,)), DMA((3, nz)), DMA((3, nz)), DMA((nz,)), DMA((nz,))]
    plain = [DMA((nz,)), DMA((nz,)), DMA((3,)), DMA((3,)), DMA((nz,)), DMA((nz,))]
    return pl.pallas_call(
        functools.partial(gather_kernel, nz),
        out_shape=(
            jax.ShapeDtypeStruct((NS, rows, model), BF16),
            jax.ShapeDtypeStruct((grp, depth, 3 * width), BF16),
            jax.ShapeDtypeStruct((NX, 2, grp) + wo.shape, BF16),
        ),
        in_specs=[ANY] * 3,
        out_specs=[ANY] * 3,
        scratch_shapes=[DMA((2,)), DMA((8, CHUNKS)), DMA((NS, CHUNKS))]
        + ring
        + [DMA((3,)), DMA((3,))]
        + ring
        + plain,
        compiler_params=pltpu.CompilerParams(collective_id=0, has_side_effects=True),
        name="gather",
    )(tok, w, wo)


def exchange_kernel(nz, att, kv, att_in, kv_in, ls, ss, rs):
    place = Place(nz)
    link = Link(place)
    s = place.s
    keep = pltpu.make_async_copy(att.at[s], att_in.at[s], ls)
    keep.start()
    barrier([place.sn(d) for d in range(1, NS)])
    for d in range(1, NS):
        to = (s + d) % NS
        link.send(att.at[to], att_in.at[s], ss.at[d], rs.at[d], {"seq": to})
    link.send(kv, kv_in, ss.at[0], rs.at[0], place.xn(2))
    for d in range(1, NS):
        link.arrived(att_in.at[(s - d + NS) % NS], ss.at[0], rs.at[d])
    link.arrived(kv_in, ss.at[0], rs.at[0])
    keep.wait()
    link.finish()


def exchange_call(nz, att, kv):
    return pl.pallas_call(
        functools.partial(exchange_kernel, nz),
        out_shape=(
            jax.ShapeDtypeStruct(att.shape, BF16),
            jax.ShapeDtypeStruct(kv.shape, BF16),
        ),
        in_specs=[ANY] * 2,
        out_specs=[ANY] * 2,
        scratch_shapes=[DMA, DMA((NS,)), DMA((NS,))],
        compiler_params=pltpu.CompilerParams(collective_id=1, has_side_effects=True),
        name="exchange",
    )(att, kv)


def head_kernel(
    nz, st, gain, embed, norm_out, max_out,
    emb, own, zbuf, rows, buf, m1, m2, m3,
    ls, s1, r1, s2, r2, s3, r3, s4, r4, s5, r5, s6, r6, s7, r7,
):
    place = Place(nz)
    link = Link(place)
    s, y, z, c = place.s, place.y, place.z, place.c
    fetch = pltpu.make_async_copy(embed, emb, ls)
    fetch.start()
    seq_peers = [place.sn(d) for d in range(1, NS)]
    y_peers = [place.yn(d) for d in range(1, NY)]
    z_peers = [place.zn(d) for d in range(1, nz)]
    barrier(seq_peers + y_peers + z_peers)
    own[s] = st[s]
    for d in range(1, NS):
        to = (s + d) % NS
        link.send(st.at[to], own.at[s], s1.at[d], r1.at[d], {"seq": to})
    for d in range(1, NS):
        link.arrived(own.at[(s - d + NS) % NS], s1.at[0], r1.at[d])
    zbuf[z] = jnp.sum(own[...], axis=0)
    for d in range(1, nz):
        link.send(zbuf.at[z], zbuf.at[z], s2.at[d], r2.at[d], place.zn(d))
    for d in range(1, nz):
        link.arrived(zbuf.at[(z - d + nz) % nz], s2.at[0], r2.at[d])
    for n in range(nz):
        rows[n * SEGS : (n + 1) * SEGS] = zbuf[n]
    buf[s, y] = rows[...].astype(BF16)
    for d in range(1, NY):
        link.send(buf.at[s, y], buf.at[s, y], s3.at[d], r3.at[d], place.yn(d))
    for d in range(1, NY):
        link.arrived(buf.at[s, (y - d + NY) % NY], s3.at[0], r3.at[d])
    link.send(buf.at[s], buf.at[s], s4.at[0], r4.at[0], place.sib)
    for d in range(1, NX):
        link.send(buf.at[s], buf.at[s], s4.at[d], r4.at[d], place.xn(d))
    for d in (1, 3, 2):
        came = buf.at[place.xs(-d)]
        link.arrived(came, s4.at[0], r4.at[d])
        link.send(came, came, s5.at[d], r5.at[d], place.sib)
    for d in range(NX):
        came = buf.at[2 * ((place.x - d + NX) % NX) + 1 - c]
        link.arrived(came, s4.at[0], r4.at[0] if d == 0 else r5.at[d])
    count = NY * nz * SEGS
    width = buf.shape[-1]
    total = jnp.zeros((count, 1), F32)
    for n in range(NS):
        value = buf[n].reshape(count, width).astype(F32)
        total = total + jnp.sum(value * value, axis=1, keepdims=True)
    mean = total / (NS * width)
    norm_out[...] = jnp.sqrt(mean)
    scale = lax.rsqrt(mean + eps)
    fetch.wait()
    logits = jnp.zeros((emb.shape[0], count), F32)
    for n in range(NS):
        value = buf[n].reshape(count, width).astype(F32)
        final = (value * scale * gain[:, n * width : (n + 1) * width]).astype(BF16)
        logits = logits + lax.dot_general(
            emb[:, n * width : (n + 1) * width],
            final,
            (((1,), (1,)), ((), ())),
            preferred_element_type=F32,
        )
    m1[s] = jnp.max(logits, axis=0, keepdims=True)
    for d in range(1, NS):
        link.send(m1.at[s], m1.at[s], s6.at[d], r6.at[d], place.sn(d))
    for d in range(1, NS):
        link.arrived(m1.at[(s - d + NS) % NS], s6.at[0], r6.at[d])
    m2[y] = jnp.max(m1[...], axis=0)
    for d in range(1, NY):
        link.send(m2.at[y], m2.at[y], s7.at[d], r7.at[d], place.yn(d))
    for d in range(1, NY):
        link.arrived(m2.at[(y - d + NY) % NY], s7.at[0], r7.at[d])
    m3[z] = jnp.max(m2[...], axis=0)
    for d in range(1, nz):
        link.send(m3.at[z], m3.at[z], s7.at[NY + d], r7.at[NY + d], place.zn(d))
    for d in range(1, nz):
        link.arrived(m3.at[(z - d + nz) % nz], s7.at[0], r7.at[NY + d])
    max_out[...] = cap_value * jnp.tanh(jnp.max(m3[...], axis=0) / cap_value)
    link.finish()


def head_call(nz, st, gain, embed):
    count = NY * nz * SEGS
    width = st.shape[-1]
    return pl.pallas_call(
        functools.partial(head_kernel, nz),
        out_shape=(
            jax.ShapeDtypeStruct((count, 1), F32),
            jax.ShapeDtypeStruct((1, count), F32),
        ),
        in_specs=[VMEM, VMEM, ANY],
        out_specs=[VMEM, VMEM],
        scratch_shapes=[
            pltpu.VMEM(embed.shape, BF16),
            pltpu.VMEM((NS, SEGS, width), F32),
            pltpu.VMEM((nz, SEGS, width), F32),
            pltpu.VMEM((nz * SEGS, width), F32),
            pltpu.VMEM((NS, NY, nz * SEGS, width), BF16),
            pltpu.VMEM((NS, 1, count), F32),
            pltpu.VMEM((NY, 1, count), F32),
            pltpu.VMEM((nz, 1, count), F32),
            DMA,
            DMA((NS,)), DMA((NS,)),
            DMA((nz,)), DMA((nz,)),
            DMA((NY,)), DMA((NY,)),
            DMA((NX,)), DMA((NX,)),
            DMA((NX,)), DMA((NX,)),
            DMA((NS,)), DMA((NS,)),
            DMA((NY + nz,)), DMA((NY + nz,)),
        ],
        compiler_params=pltpu.CompilerParams(
            collective_id=2, has_side_effects=True, vmem_limit_bytes=32 * 1024 * 1024
        ),
        name="head",
    )(st, gain, embed)


def rows_scaled(value_rows, scales):
    mean_square = jnp.mean(value_rows * value_rows, axis=-1, keepdims=True)
    return value_rows * lax.rsqrt(mean_square + eps) * scales


def rotate(value_rows, offsets):
    half_width = value_rows.shape[-1] // 2
    frequency = rope_base ** (
        -2.0 * jnp.arange(half_width, dtype=F32) / value_rows.shape[-1]
    )
    angles = offsets.astype(F32)[:, None] * frequency[None, :]
    cosine, sine = jnp.cos(angles), jnp.sin(angles)
    lower, upper = value_rows[:, :half_width], value_rows[:, half_width:]
    return jnp.concatenate(
        [lower * cosine - upper * sine, upper * cosine + lower * sine], axis=-1
    )


def shards(
    tokens, seg_ids, deal, page_table, in_gain, w_query, key_weight, value_weight,
    q_gain, key_gain, w_out, post_gain, final_gain, embed,
):
    nz = lax.axis_size("grp") // NY
    own_tokens = tokens[0]
    rows, model = own_tokens.shape
    segment, pos = seg_ids[0], deal[0]
    pack = pos.shape[0]
    width = q_gain.shape[0]
    s = lax.axis_index("seq")
    own_start = s * rows

    normed = rows_scaled(own_tokens.astype(F32), in_gain).astype(BF16)
    group = s // (NS // KEY_HEADS) * width
    w_key = lax.dynamic_slice_in_dim(key_weight, group, width, 1)
    w_value = lax.dynamic_slice_in_dim(value_weight, group, width, 1)
    even = s % 2 == 0
    w_own = jnp.concatenate(
        [jnp.where(even, w_key, w_query), jnp.where(even, w_query, w_value)], axis=1
    )
    tok_all, w_all, wo_all = gather_call(nz, normed, w_own, w_out.T)

    ends = jnp.sum(
        (segment[None, :] <= jnp.arange(SEGS, dtype=jnp.int32)[:, None]).astype(jnp.int32), axis=1
    )
    start = jnp.max(jnp.where(pos[:, None] >= ends[None, :], ends[None, :], 0), axis=1)
    offsets = pos - start

    raw = jnp.dot(
        tok_all.reshape(pack, model), w_all.reshape(model, 3 * width), preferred_element_type=F32
    )
    key = rotate(rows_scaled(raw[:, :width], key_gain), offsets).astype(BF16)
    query = rotate(rows_scaled(raw[:, width : 2 * width], q_gain), offsets).astype(BF16)
    value = rows_scaled(raw[:, 2 * width :], 1.0).astype(BF16)

    scores = lax.dot_general(query, key, (((1,), (1,)), ((), ())), preferred_element_type=F32)
    allowed = (pos[None, :] <= pos[:, None]) & (pos[None, :] >= start[:, None])
    masked = jnp.where(allowed, scores, -1e30)
    peak = jnp.max(masked, axis=-1, keepdims=True)
    raw_weights = jnp.where(allowed, jnp.exp(masked - peak), 0.0)
    total = jnp.sum(raw_weights, axis=-1, keepdims=True)
    weights = (raw_weights / total).astype(BF16)
    attended = jnp.dot(weights, value, preferred_element_type=F32).astype(BF16)

    pages = page_table[0]
    slots_page = pack // pages.shape[0]
    page_of = jnp.sum(
        jnp.where(
            (pos // slots_page)[:, None] == jnp.arange(pages.shape[0], dtype=jnp.int32)[None, :],
            pages[None, :],
            0,
        ),
        axis=1,
    )
    physical = page_of * slots_page + pos % slots_page
    both = jnp.concatenate([key, value], axis=1)
    partner = (s + NS // 2) % NS
    target = jnp.concatenate(
        [own_start + jnp.arange(rows, dtype=jnp.int32), partner * rows + jnp.arange(rows, dtype=jnp.int32)]
    )
    pick = (target[:, None] == physical[None, :]).astype(BF16)
    picked = jnp.dot(pick, both, preferred_element_type=F32).astype(BF16)

    att_in, kv_in = exchange_call(nz, attended.reshape(NS, rows, width), picked[rows:])
    first = s < NS // 2
    low = jnp.where(first, picked[:rows], kv_in)
    high = jnp.where(first, kv_in, picked[:rows])
    cache = jnp.concatenate(
        [low[:, :width], high[:, :width], low[:, width:], high[:, width:]], axis=1
    ).reshape(rows // slots_page, slots_page, 2 * KEY_HEADS * width)

    wo = wo_all.reshape(NS, model, width)
    summed = jnp.zeros((rows, model), F32)
    for n in range(NS):
        part = lax.dot_general(
            att_in[n], wo[n], (((1,), (1,)), ((), ())), preferred_element_type=F32
        )
        summed = summed + part.astype(BF16).astype(F32)
    hidden = (own_tokens.astype(F32) + rows_scaled(summed, post_gain)).astype(BF16)

    own_pos = lax.dynamic_slice_in_dim(pos, own_start, rows, 0)
    selector = (own_pos[None, :] == (ends - 1)[:, None]).astype(BF16)
    states = jnp.dot(selector, hidden, preferred_element_type=F32)
    states = states.reshape(SEGS, NS, width).transpose(1, 0, 2)
    norm, top = head_call(nz, states, final_gain[None, :], embed)
    order = lambda v: v.reshape(NY, nz, SEGS).transpose(1, 0, 2).reshape(-1)
    return (hidden[None], cache[None], order(norm), order(top))


def solution(mesh):
    return jax.shard_map(
        shards,
        mesh=mesh,
        in_specs=(
            P("grp", "seq", None),
            P("grp", None),
            P("grp", None),
            P("grp", None),
            P(),
            P("grp", "seq"),
            P("grp", None),
            P("grp", None),
            P(),
            P(),
            P("seq", "grp"),
            P(),
            P(),
            P(("grp", "seq"), None),
        ),
        out_specs=(P("grp", "seq", None), P("grp", "seq", None, None), P(), P()),
        check_vma=False,
    )
```

time: 1010 us -> 186 us (0.18)
  waiting for transfers between devices: 782 us -> 0 us
  Pallas kernels: 0 us -> 145 us
  blocking collectives: 134 us -> 0 us
  local copies, waits for them, and re-layouts: 36.2 us -> 2.87 us
  between operations: 14.2 us -> 1.07 us
  other arithmetic: 22.9 us -> 11.8 us
    all_gather x8 -> x0, waiting for transfers between devices: 739 us -> none  [the longest x1 132 us: shards(): lax.all_gather(value_projection_weight, 'grp', axis=0, tiled=True)]
    pallas_call x0 -> x3, Pallas kernels: none -> 145 us  [the longest x1 86.3 us: gather_call(): pl.pallas_call(functools.partial(gather_kernel, nz), out_shape=(jax.Shape...]
    pmax x1 -> x0, blocking collectives: 110 us -> none  [shards(): max_logit = lax.pmax(shard_max, ('grp', 'seq'))]
    reduce_scatter x1 -> x0, waiting for transfers between devices: 40.6 us -> none  [shards(): lax.psum_scatter(partial_out.astype(jnp.bfloat16), 'seq', scatter_dimensi...]
    psum x1 -> x0, blocking collectives: 24.1 us -> none  [shards(): pack_states = lax.psum(group_states.astype(jnp.bfloat16), 'seq')]
    gather x6 -> x0, local copies, waits for them, and re-layouts: 11 us -> none  [the longest x1 5.72 us: layout(): row_seg = jnp.take(segment, dealing)]
    dot_general x7 -> x13, matrix products: 21.4 us -> 24.7 us  [the longest x8 14.1 us: shards(): lax.dot_general(att_in[n], wo[n], (((1,), (1,)), ((), ())), preferred_ele...]
  transfers between devices with their start and end apart: 9 -> 0, of which waited for: 9 -> 0; matrix products, arithmetic and copies ran while one was open for 6% -> 0% of each run, Pallas kernels for 0% -> 0%
where the time goes in v1:
time: 186 us; the launch traced here: 185 us
  Pallas kernels  145 us (78%)
  matrix products  24.7 us (13%)
  other arithmetic  11.8 us (6%)
  local copies, waits for them, and re-layouts  2.87 us (2%)
    pallas_call x1, Pallas kernels, gather_call(): pl.pallas_call(functools.partial(gather_kernel, nz), out_shape=(jax.Shape...  86.3 us
    pallas_call x1, Pallas kernels, head_call(): pl.pallas_call(functools.partial(head_kernel, nz), out_shape=(jax.ShapeDt...  45 us
    dot_general x8, matrix products, shards(): lax.dot_general(att_in[n], wo[n], (((1,), (1,)), ((), ())), preferred_ele...  14.1 us
    pallas_call x1, Pallas kernels, exchange_call(): pl.pallas_call(functools.partial(exchange_kernel, nz), out_shape=(jax.Sha...  13.4 us
    dot_general x1, matrix products, shards(): jnp.dot(tok_all.reshape(pack, model), w_all.reshape(model, 3 * width), pr...  6.41 us

profile of v1, /device:TPU:1, one launch (start us, length us, event | category | flops | bytes accessed | tf_op | source)
XLA Modules:
  0.0 185.0 jit_solution(16147744059335722837)
XLA Ops:
  0.6 1.2 fusion.19
  1.9 2.0 %fusion.21.tok = bf16[128,2048]{1,0:T(8,128)(2,1)} fusion(bf16[1,128,2048]{2,1,0:T(8,128)(2,1)} %param.14, f32[2048]{0:T(1024)} %param.18, f32[128]{0:T(128)S(1)} %add_rsqrt_fusion.4), kind=kLoop, calls=%fused_computation.36 | loop fusion | flops 1048576 | bytes 1057280 | tf_op jit(solution)/shard_map/convert_element_type | solution.py:468
  3.9 0.8 dynamic-slice_select_fusion.1
  4.7 0.6 pad_maximum_fusion.w
  5.3 86.3 %gather.1 = (bf16[8,128,2048]{2,1,0:T(8,128)(2,1)}, bf16[64,32,768]{2,1,0:T(8,128)(2,1)}, bf16[4,2,64,32,256]{4,3,2,1,0:T(8,128)(2,1)}) custom-call(bf16[128,2048]{1,0:T(8,128)(2,1)} %fusion.21.tok, bf16[32,512]{1,0:T(8,128)(2,1)} %pad_maximum_fusion.w, bf16[32,256]{1,0:T(8,128)(2,1)} %bitcast.101), custom_call_target="tpu_custom_call" | custom-call | tf_op jit(solution)/shard_map/gather/pallas_call | solution.py:268
  91.6 6.4 %fusion.86 = f32[1024,768]{0,1:T(8,128)S(1)} fusion(bf16[1024,2048]{1,0:T(8,128)(2,1)} %bitcast.106, bf16[2048,768]{1,0:T(8,128)(2,1)} %bitcast.107), kind=kOutput, calls=%fused_computation.150 | convolution fusion | flops 3221225472 | bytes 10485760 | tf_op jit(solution)/shard_map/dot_general | solution.py:484
  98.0 0.3 multiply_reduce_fusion.2
  98.4 0.3 multiply_multiply_fusion
  99.0 2.4 %fusion.43 = (bf16[1024,128]{0,1:T(8,128)(2,1)S(1)}, bf16[1024,128]{0,1:T(8,128)(2,1)S(1)}, bf16[1024,128]{0,1:T(8,128)(2,1)S(1)}, bf16[1024,128]{0,1:T(8,128)(2,1)S(1)}) fusion(f32[1024,256]{0,1:T(8,128)S(1)} %get-tuple-element.21, f32[128]{0:T(128)S(1)} %multiply_power_fusion, f32[1024]{0:T(1024)S(1)} %get-tuple-element.39, ...), kind=kLoop, calls=%fused_computation.75 | loop fusion | flops 2228224 | bytes 3150336 | tf_op jit(solution)/shard_map/convert.1
  101.5 1.0 fusion.1
  102.5 1.6 fusion.37
  104.0 2.5 %fusion.18 = bf16[1024,256]{1,0:T(8,128)(2,1)} fusion(bf16[1024,256]{0,1:T(8,128)(2,1)S(1)} %get-tuple-element.22, f32[1024]{0:T(1024)S(1)} %fusion.37, f32[1024,1024]{0,1:T(8,128)S(1)} %get-tuple-element.41, f32[1024]{0:T(1024)S(1)} %get-tuple-element.40, s32[1024]{0:T(1024)S(1)} %select_reduce_fusion.1, s32[1024]{0:T(1024)S(1)} %bitcast.100), kind=kOutput, calls=%fused_computation.32 | convolution fusion | flops 545521664 | bytes 5259264 | tf_op jit(solution)/shard_map/dot_general | solution.py:498
  106.5 0.4 select_reduce_fusion
  106.9 0.5 convolution_convert_fusion.8
  107.4 0.7 slice.124.kv
  108.1 13.4 %exchange.1 = (bf16[8,128,256]{2,1,0:T(8,128)(2,1)}, bf16[128,512]{1,0:T(8,128)(2,1)}) custom-call(bf16[8,128,256]{2,1,0:T(8,128)(2,1)} %bitcast.93, bf16[128,512]{1,0:T(8,128)(2,1)} %slice.124.kv), custom_call_target="tpu_custom_call" | custom-call | tf_op jit(solution)/shard_map/exchange/pallas_call | solution.py:306
  121.5 1.8 fusion.16
  123.3 1.7 fusion.15
  125.1 1.7 fusion.13
  126.8 1.7 fusion.11
  128.5 1.7 fusion.9
  130.3 1.8 fusion.7
  132.0 1.7 fusion.5
  133.8 1.9 %multiply_reduce_fusion = (f32[128]{0:T(128)S(1)}, f32[128,2048]{1,0:T(8,128)S(1)}) fusion(f32[128,2048]{1,0:T(8,128)S(1)} %fusion.5, bf16[8,2048,256]{2,1,0:T(8,128)(2,1)} %bitcast.91, bf16[8,128,256]{2,1,0:T(8,128)(2,1)S(1)} %copy-done.4), kind=kOutput, calls=%fused_computation.51 | convolution fusion | flops 135528320 | bytes 3211776 | tf_op jit(solution)/shard_map/dot_general | solution.py:530
  135.8 0.2 fusion.22
  136.1 0.8 maximum_bitcast_fusion
  136.9 0.2 fusion.75
  137.1 45.0 %head.1 = (f32[256,1]{1,0:T(8,128)S(1)}, f32[1,256]{1,0:T(1,128)S(1)}) custom-call(f32[8,4,256]{2,1,0:T(4,128)S(1)} %bitcast.82, f32[1,2048]{1,0:T(1,128)S(1)} %bitcast.83, bf16[512,2048]{1,0:T(8,128)(2,1)S(1)} %copy-done), custom_call_target="tpu_custom_call" | custom-call | tf_op jit(solution)/shard_map/head/pallas_call | solution.py:404
  182.4 0.7 reshape.148
  183.0 0.5 broadcast.184
  183.5 0.7 reduce.4
  184.3 0.7 reshape.150
  (46 shorter events, 0.8 us)
Async XLA Ops:
  91.6 6.8 %copy-start.9 = (f32[256]{0:T(256)S(1)}, f32[256]{0:T(256)}, u32[]{:S(2)}) copy-start(f32[256]{0:T(256)} %param.23) | copy-start | bytes 3076
  91.6 6.8 %copy-start.10 = (f32[256]{0:T(256)S(1)}, f32[256]{0:T(256)}, u32[]{:S(2)}) copy-start(f32[256]{0:T(256)} %param.22) | copy-start | bytes 3076
  98.0 0.8 copy-start.8
  98.0 0.9 copy-start.6
  104.0 2.5 %copy-start.11 = (s32[1,128]{1,0:T(1,128)S(1)}, s32[1,128]{1,0:T(1,128)}, u32[]{:S(2)}) copy-start(s32[1,128]{1,0:T(1,128)} %param.17) | copy-start | bytes 1540
  121.5 3.6 %copy-start.4 = (bf16[8,128,256]{2,1,0:T(8,128)(2,1)S(1)}, bf16[8,128,256]{2,1,0:T(8,128)(2,1)}, u32[]{:S(2)}) copy-start(bf16[8,128,256]{2,1,0:T(8,128)(2,1)} %get-tuple-element.13) | copy-start | bytes 1572868
  130.2 5.5 %copy-start.2 = (bf16[1,128,2048]{2,1,0:T(8,128)(2,1)S(1)}, bf16[1,128,2048]{2,1,0:T(8,128)(2,1)}, u32[]{:S(2)}) copy-start(bf16[1,128,2048]{2,1,0:T(8,128)(2,1)} %param.14) | copy-start | bytes 1572868
  130.2 5.5 %copy-start.7 = (f32[2048]{0:T(1024)S(1)}, f32[2048]{0:T(1024)}, u32[]{:S(2)}) copy-start(f32[2048]{0:T(1024)} %param.25) | copy-start | bytes 24580
  132.0 4.0 %copy-start.5 = (bf16[128,512]{1,0:T(8,128)(2,1)S(1)}, bf16[128,512]{1,0:T(8,128)(2,1)}, u32[]{:S(2)}) copy-start(bf16[128,512]{1,0:T(8,128)(2,1)} %get-tuple-element.15) | copy-start | bytes 393220
  133.8 3.4 %copy-start = (bf16[512,2048]{1,0:T(8,128)(2,1)S(1)}, bf16[512,2048]{1,0:T(8,128)(2,1)}, u32[]{:S(2)}) copy-start(bf16[512,2048]{1,0:T(8,128)(2,1)} %embed.1) | copy-start | bytes 6291460
  133.8 3.3 %copy-start.1 = (f32[2048]{0:T(1024)S(1)}, f32[2048]{0:T(1024)}, u32[]{:S(2)}) copy-start(f32[2048]{0:T(1024)} %param.26) | copy-start | bytes 24580
  136.0 49.0 %copy-start.3 = (bf16[128,2048]{1,0:T(8,128)(2,1)}, bf16[128,2048]{1,0:T(8,128)(2,1)S(1)}, u32[]{:S(2)}) copy-start(bf16[128,2048]{1,0:T(8,128)(2,1)S(1)} %fusion.22) | copy-start | bytes 1572868

commit v2 on v1

v2 whole, which is shorter than its diff:
```python
import functools

import jax
import jax.numpy as jnp
from jax import lax
from jax.experimental import pallas as pl
from jax.experimental.pallas import tpu as pltpu
from jax.sharding import PartitionSpec as P

MESH = pl.DeviceIdType.MESH
ANY = pl.BlockSpec(memory_space=pl.ANY)
VMEM = pl.BlockSpec(memory_space=pltpu.VMEM)
BF16 = jnp.bfloat16
F32 = jnp.float32
DMA = pltpu.SemaphoreType.DMA

KEY_HEADS = 2
PAGE_SLOTS = 8
SEGS = 4
NY = 4
NX = 4
NS = 8
CHUNKS = 4
eps = 1e-06
rope_base = 1000000.0
cap_value = 30.0


def remote(src, dst, send_sem, recv_sem, device):
    return pltpu.make_async_remote_copy(
        src_ref=src,
        dst_ref=dst,
        send_sem=send_sem,
        recv_sem=recv_sem,
        device_id=device,
        device_id_type=MESH,
    )


class Place:
    def __init__(self, nz):
        self.nz = nz
        self.g = lax.axis_index("grp")
        self.s = lax.axis_index("seq")
        self.z, self.y = self.g // NY, self.g % NY
        self.x, self.c = self.s // 2, self.s % 2
        self.sib = {"seq": 2 * self.x + 1 - self.c}

    def zn(self, d):
        return {"grp": ((self.z + d + self.nz) % self.nz) * NY + self.y}

    def yn(self, d):
        return {"grp": self.z * NY + (self.y + d + NY) % NY}

    def xs(self, d):
        return 2 * ((self.x + d + NX) % NX) + self.c

    def xn(self, d):
        return {"seq": self.xs(d)}

    def sn(self, d):
        return {"seq": (self.s + d) % NS}


class Link:
    def __init__(self, place):
        self.place = place
        self.sent = []

    def send(self, src, dst, send_sem, recv_sem, device):
        copy = remote(src, dst, send_sem, recv_sem, device)
        copy.start()
        self.sent.append(copy)

    def arrived(self, dst, send_sem, recv_sem):
        remote(dst, dst, send_sem, recv_sem, self.place.sib).wait_recv()

    def finish(self):
        for copy in self.sent:
            copy.wait_send()


def slots(place, k):
    nz = place.nz
    half = nz // 2
    if k == 0:
        return [(0, place.z, 1)]
    if k > half:
        return []
    up = (k, (place.z - k + nz) % nz, 1)
    if k == half:
        return [up]
    return [up, (half + k, (place.z + k) % nz, -1)]


def gather_rows(place, link, every, ss, rs):
    step = every.shape[1] // CHUNKS
    piece = lambda s, j: every.at[s, pl.ds(j * step, step)]
    s, left, right, far = place.s, place.xs(-1), place.xs(1), place.xs(2)
    for j in range(CHUNKS):
        mine = piece(s, j)
        link.send(mine, mine, ss.at[0, j], rs.at[s, j], place.xn(1))
        link.send(mine, mine, ss.at[1, j], rs.at[s, j], place.xn(-1))
    for j in range(CHUNKS):
        link.send(piece(s, j), piece(s, j), ss.at[2, j], rs.at[s, j], place.sib)
    yield
    for j in range(CHUNKS):
        link.arrived(piece(left, j), ss.at[0, 0], rs.at[left, j])
        if 2 * j < CHUNKS:
            link.send(piece(left, j), piece(left, j), ss.at[3, j], rs.at[left, j], place.xn(1))
        link.send(piece(left, j), piece(left, j), ss.at[4, j], rs.at[left, j], place.sib)
        link.arrived(piece(right, j), ss.at[0, 0], rs.at[right, j])
        if 2 * j >= CHUNKS:
            link.send(piece(right, j), piece(right, j), ss.at[3, j], rs.at[right, j], place.xn(-1))
        link.send(piece(right, j), piece(right, j), ss.at[5, j], rs.at[right, j], place.sib)
        yield
    for j in range(CHUNKS):
        link.arrived(piece(far, j), ss.at[0, 0], rs.at[far, j])
        link.send(piece(far, j), piece(far, j), ss.at[6, j], rs.at[far, j], place.sib)
        yield
    for x in range(NX):
        other = 2 * x + 1 - place.c
        for j in range(CHUNKS):
            link.arrived(piece(other, j), ss.at[0, 0], rs.at[other, j])


def gather_zy(place, link, block, plane, other_plane, sems):
    zs, zr, ys, yr, ss, sr = sems
    half = place.nz // 2
    gy = lambda z, d: z * NY + (place.y + d + NY) % NY
    for k in range(half + 3):
        for q, z, way in slots(place, k):
            here = block(gy(z, 0))
            if k > 0:
                link.arrived(here, zs.at[q], zr.at[q])
            if k == 0:
                link.send(here, here, zs.at[1], zr.at[1], place.zn(1))
                if half > 1:
                    link.send(here, here, zs.at[half + 1], zr.at[half + 1], place.zn(-1))
            elif way == 1 and k < half:
                link.send(here, here, zs.at[q + 1], zr.at[q + 1], place.zn(1))
            elif way == -1 and k < half - 1:
                link.send(here, here, zs.at[q + 1], zr.at[q + 1], place.zn(-1))
            link.send(here, here, ys.at[0, q], yr.at[0, q], place.yn(1))
            link.send(here, here, ys.at[1, q], yr.at[1, q], place.yn(-1))
        for q, z, way in slots(place, k - 1) if k >= 1 else []:
            near = block(gy(z, -way))
            kind = 0 if way == 1 else 1
            link.arrived(near, zs.at[0], yr.at[kind, q])
            link.send(near, near, ys.at[2, q], yr.at[2, q], place.yn(way))
        for q, z, way in slots(place, k - 2) if k >= 2 else []:
            link.arrived(block(gy(z, way)), zs.at[0], yr.at[1 if way == 1 else 0, q])
            link.arrived(block(gy(z, 2)), zs.at[0], yr.at[2, q])
            link.send(plane(z), plane(z), ss.at[q], sr.at[q], place.sib)
        yield
    for k in range(half + 1):
        for q, z, way in slots(place, k):
            link.arrived(other_plane(z), zs.at[0], sr.at[q])


def gather_yz(place, link, block, plane, other_plane, sems):
    zs, zr, ys, yr, ss, sr = sems
    half = place.nz // 2
    gy = lambda d: place.z * NY + (place.y + d + NY) % NY
    here = block(gy(0))
    link.send(here, here, ys.at[0], yr.at[0], place.yn(1))
    link.send(here, here, ys.at[1], yr.at[1], place.yn(-1))
    yield
    near = block(gy(-1))
    link.arrived(near, zs.at[0], yr.at[0])
    link.send(near, near, ys.at[2], yr.at[2], place.yn(1))
    link.arrived(block(gy(1)), zs.at[0], yr.at[1])
    link.arrived(block(gy(2)), zs.at[0], yr.at[2])
    for k in range(half + 1):
        for q, z, way in slots(place, k):
            here = plane(z)
            if k > 0:
                link.arrived(here, zs.at[q], zr.at[q])
            if k == 0:
                link.send(here, here, zs.at[1], zr.at[1], place.zn(1))
                if half > 1:
                    link.send(here, here, zs.at[half + 1], zr.at[half + 1], place.zn(-1))
            elif way == 1 and k < half:
                link.send(here, here, zs.at[q + 1], zr.at[q + 1], place.zn(1))
            elif way == -1 and k < half - 1:
                link.send(here, here, zs.at[q + 1], zr.at[q + 1], place.zn(-1))
            link.send(here, here, ss.at[q], sr.at[q], place.sib)
        yield
    for k in range(half + 1):
        for q, z, way in slots(place, k):
            link.arrived(other_plane(z), zs.at[0], sr.at[q])


def together(gens):
    gens = list(gens)
    while gens:
        for gen in list(gens):
            if next(gen, "end") == "end":
                gens.remove(gen)
        yield


def pump(gen, steps):
    for _ in range(steps):
        next(gen, None)


def scaled(value, gain):
    mean_square = jnp.mean(value * value, axis=-1, keepdims=True)
    value = value * lax.rsqrt(mean_square + eps)
    return value if gain is None else value * gain


def rotated(value, cosine, sine):
    half = value.shape[-1] // 2
    lower, upper = value[:, :half], value[:, half:]
    return jnp.concatenate(
        [lower * cosine - upper * sine, upper * cosine + lower * sine], axis=-1
    )


def column(row):
    return jnp.broadcast_to(row, (128, 128)).T


def nt(a, b):
    return lax.dot_general(a, b, (((1,), (1,)), ((), ())), preferred_element_type=F32)


def whole_kernel(
    nz,
    tok, seg, pos, pages, in_gain, freq, wq, wk, wv, wo, q_gain, k_gain, post_gain, final_gain, embed,
    hidden_out, cache_out, norm_out, max_out,
    v, d,
):
    place = Place(nz)
    link = Link(place)
    g, s, x, y, z, c = place.g, place.s, place.x, place.y, place.z, place.c
    rows, model = tok.shape
    width = q_gain.shape[1]
    pack = pos.shape[1]
    lanes = lambda start, size: pl.ds(pl.multiple_of(start, 128), size)

    fetch = pltpu.make_async_copy(embed, v.emb, d.fetch)
    fetch.start()
    peers = (
        [place.sn(n) for n in range(1, NS)]
        + [place.yn(n) for n in range(1, NY)]
        + [place.zn(n) for n in range(1, nz)]
    )
    entry = pltpu.get_barrier_semaphore()
    for peer in peers:
        pl.semaphore_signal(entry, inc=1, device_id=peer, device_id_type=MESH)

    kv = jnp.where(c == 0, wk[:, lanes(x // 2 * width, width)], wv[:, lanes(x // 2 * width, width)])
    v.w_all[g, :, width : 2 * width] = wq[...]
    v.w_all[g, :, lanes(c * 2 * width, width)] = kv
    v.wo_all[x, c, g] = wo[...]
    v.tok_all[s] = scaled(tok[...].astype(F32), in_gain[...]).astype(BF16)
    segment = seg[...]
    position = pos[...].astype(F32)
    ends = [
        jnp.sum((segment <= j).astype(F32), axis=1, keepdims=True) for j in range(SEGS)
    ]
    start = jnp.zeros_like(position)
    for end in ends[:-1]:
        start = jnp.maximum(start, jnp.where(position >= end, end, 0.0))
    for n in range(pack // 128):
        block = slice(n * 128, (n + 1) * 128)
        pos_col, start_col = column(position[:, block]), column(start[:, block])
        v.pos_col[block], v.start_col[block] = pos_col, start_col
        angle = (pos_col - start_col) * freq[...]
        v.cos[block], v.sin[block] = jnp.cos(angle), jnp.sin(angle)

    pl.semaphore_wait(entry, len(peers))

    block = lambda g: v.w_all.at[g, :, lanes(c * width, 2 * width)]
    plane = lambda c: lambda z: v.w_all.at[pl.ds(z * NY, NY), :, lanes(c * 2 * width, width)]
    wo_block = lambda n: lambda g: v.wo_all.at[n, c, g]
    wo_plane = lambda n, c: lambda z: v.wo_all.at[n, c, pl.ds(z * NY, NY)]

    def flow(n, way):
        return way(place, link, wo_block(n), wo_plane(n, c), wo_plane(n, 1 - c), d.wo[n])

    first = together([
        gather_zy(place, link, block, plane(c), plane(1 - c), d.w),
        gather_rows(place, link, v.tok_all, d.ts, d.tr),
    ])
    next(first)
    own = v.wo_all.at[x, c, g]
    for n, way in enumerate((1, -1, 2)):
        link.send(own, own, d.xs.at[n], d.xr.at[n], place.xn(way))
    next(first)
    for n, way in enumerate((1, -1, 2)):
        link.arrived(v.wo_all.at[(x - way + NX) % NX, c, g], d.xs.at[0], d.xr.at[n])
    early = flow(0, gather_yz)
    for _ in first:
        pump(early, 1)
    late = together([flow(1, gather_yz), flow(2, gather_zy), flow(3, gather_zy)])
    background = together([early, late])

    pump(background, 1)
    rest = v.w_all[...].reshape(model, 3 * width)
    part = 4
    for n in range(NS // part):
        here = slice(n * part * rows, (n + 1) * part * rows)
        raw = jnp.dot(
            v.tok_all[n * part : (n + 1) * part].reshape(part * rows, model),
            rest,
            preferred_element_type=F32,
        )
        cosine, sine = v.cos[here], v.sin[here]
        key = rotated(scaled(raw[:, :width], k_gain[...]), cosine, sine)
        query = rotated(scaled(raw[:, width : 2 * width], q_gain[...]), cosine, sine)
        v.query[here] = query.astype(BF16)
        v.kv[here, :width] = key.astype(BF16)
        v.kv[here, width:] = scaled(raw[:, 2 * width :], None).astype(BF16)
        pump(background, 1)

    for n, way in enumerate((2, 1, -1, 0)):
        chip = (x + way + NX) % NX
        here = pl.ds(pl.multiple_of(chip * 2 * rows, 256), 2 * rows)
        scores = nt(v.query[here], v.kv[:, :width])
        allowed = (position <= v.pos_col[here, 0:1]) & (position >= v.start_col[here, 0:1])
        masked = jnp.where(allowed, scores, -1e30)
        raw = jnp.exp(masked - jnp.max(masked, axis=1, keepdims=True))
        weights = (raw / jnp.sum(raw, axis=1, keepdims=True)).astype(BF16)
        attended = jnp.dot(weights, v.kv[:, width:], preferred_element_type=F32).astype(BF16)
        v.att[2 * chip] = attended[:rows]
        v.att[2 * chip + 1] = attended[rows:]
        there = 2 * chip + 1 - c
        link.send(v.att.at[there], v.att_in.at[s], d.asend.at[n, 0], d.arecv.at[n, 0], {"seq": there})
        if way == 0:
            v.att_in[s] = v.att[s]
        else:
            there = 2 * chip + c
            link.send(
                v.att.at[there], v.att_in.at[s], d.asend.at[n, 1], d.arecv.at[n, 1], {"seq": there}
            )
        pump(background, 2)

    table = column(pages[...].astype(F32))
    whole, within = pos[...] // PAGE_SLOTS, pos[...] % PAGE_SLOTS
    count = pages.shape[1]
    match = lax.broadcasted_iota(jnp.int32, (count, pack), 0) == whole
    page = jnp.sum(jnp.where(match, table[:, 0:1], 0.0), axis=0, keepdims=True)
    physical = page.astype(jnp.int32) * PAGE_SLOTS + within
    slot = lax.broadcasted_iota(jnp.int32, (rows, pack), 0)
    partner = (s + NS // 2) % NS
    for n, owner in enumerate((partner, s)):
        pick = (slot + owner * rows == physical).astype(BF16)
        picked = jnp.dot(pick, v.kv[...], preferred_element_type=F32).astype(BF16)
        if n == 0:
            v.kv_out[...] = picked
            link.send(v.kv_out, v.kv_in, d.ks, d.kr, {"seq": partner})
            pump(background, 1)
        else:
            mine = x // 2 * width
            cache_out[:, lanes(mine, width)] = picked[:, :width]
            cache_out[:, lanes(KEY_HEADS * width + mine, width)] = picked[:, width:]
    for _ in background:
        pass
    for n, way in enumerate((2, 1, -1, 0)):
        chip = (x - way + NX) % NX
        link.arrived(v.att_in.at[2 * chip + 1 - c], d.asend.at[0, 0], d.arecv.at[n, 0])
        if way != 0:
            link.arrived(v.att_in.at[2 * chip + c], d.asend.at[0, 0], d.arecv.at[n, 1])

    span = 512
    depth = wo.shape[0]
    for m in range(model // span):
        total = jnp.zeros((span, rows), F32)
        for n in range(NS):
            w = v.wo_all[n // 2, n % 2, m * span // depth : (m + 1) * span // depth]
            total = total + nt(w.reshape(span, width), v.att_in[n]).astype(BF16).astype(F32)
        for n in range(span // 128):
            v.summed[:, m * span + n * 128 : m * span + (n + 1) * 128] = total[
                n * 128 : (n + 1) * 128
            ].T
    hidden = (tok[...].astype(F32) + scaled(v.summed[...], post_gain[...])).astype(BF16)
    hidden_out[...] = hidden

    own_pos = pos[:, lanes(s * rows, rows)].astype(F32)
    line = lax.broadcasted_iota(jnp.int32, (16, rows), 0)
    last = jnp.full((16, rows), -1.0, F32)
    for j in range(SEGS):
        last = jnp.where(line == j, ends[j] - 1.0, last)
    select = (last == own_pos).astype(BF16)
    states = jnp.dot(select, hidden, preferred_element_type=F32)
    for n in range(NS):
        v.st[n] = states[:SEGS, n * width : (n + 1) * width]
    v.own[s] = v.st[s]
    for n in range(1, NS):
        to = (s + n) % NS
        link.send(v.st.at[to], v.own.at[s], d.s1.at[n], d.r1.at[n], {"seq": to})
    link.arrived(v.kv_in, d.ks, d.kr)
    other = (1 - x // 2) * width
    cache_out[:, lanes(other, width)] = v.kv_in[:, :width]
    cache_out[:, lanes(KEY_HEADS * width + other, width)] = v.kv_in[:, width:]
    for n in range(1, NS):
        link.arrived(v.own.at[(s - n + NS) % NS], d.s1.at[0], d.r1.at[n])
    v.zbuf[z] = jnp.sum(v.own[...], axis=0)
    for n in range(1, nz):
        link.send(v.zbuf.at[z], v.zbuf.at[z], d.s2.at[n], d.r2.at[n], place.zn(n))
    for n in range(1, nz):
        link.arrived(v.zbuf.at[(z - n + nz) % nz], d.s2.at[0], d.r2.at[n])
    for n in range(nz):
        v.rows[n * SEGS : (n + 1) * SEGS] = v.zbuf[n]
    v.buf[s, y] = v.rows[...].astype(BF16)
    for n in range(1, NY):
        link.send(v.buf.at[s, y], v.buf.at[s, y], d.s3.at[n], d.r3.at[n], place.yn(n))
    for n in range(1, NY):
        link.arrived(v.buf.at[s, (y - n + NY) % NY], d.s3.at[0], d.r3.at[n])
    for n in range(1, NX):
        link.send(v.buf.at[s], v.buf.at[s], d.s4.at[n], d.r4.at[n], place.xn(n))
    link.send(v.buf.at[s], v.buf.at[s], d.s4.at[0], d.r4.at[0], place.sib)
    for n in (1, 3, 2):
        came = v.buf.at[place.xs(-n)]
        link.arrived(came, d.s4.at[0], d.r4.at[n])
        link.send(came, came, d.s5.at[n], d.r5.at[n], place.sib)
    for n in range(NX):
        came = v.buf.at[2 * ((x - n + NX) % NX) + 1 - c]
        link.arrived(came, d.s4.at[0], d.r4.at[0] if n == 0 else d.r5.at[n])
    count = NY * nz * SEGS
    total = jnp.zeros((count, 1), F32)
    for n in range(NS):
        value = v.buf[n].reshape(count, width).astype(F32)
        total = total + jnp.sum(value * value, axis=1, keepdims=True)
    mean = total / model
    norm_out[...] = jnp.sqrt(mean)
    scale = lax.rsqrt(mean + eps)
    fetch.wait()
    logits = jnp.zeros((v.emb.shape[0], count), F32)
    for n in range(NS):
        value = v.buf[n].reshape(count, width).astype(F32)
        final = (value * scale * final_gain[:, n * width : (n + 1) * width]).astype(BF16)
        logits = logits + nt(v.emb[:, n * width : (n + 1) * width], final)
    v.m1[s] = jnp.max(logits, axis=0, keepdims=True)
    for n in range(1, NS):
        link.send(v.m1.at[s], v.m1.at[s], d.s6.at[n], d.r6.at[n], place.sn(n))
    for n in range(1, NS):
        link.arrived(v.m1.at[(s - n + NS) % NS], d.s6.at[0], d.r6.at[n])
    v.m2[y] = jnp.max(v.m1[...], axis=0)
    for n in range(1, NY):
        link.send(v.m2.at[y], v.m2.at[y], d.s7.at[n], d.r7.at[n], place.yn(n))
    for n in range(1, NY):
        link.arrived(v.m2.at[(y - n + NY) % NY], d.s7.at[0], d.r7.at[n])
    v.m3[z] = jnp.max(v.m2[...], axis=0)
    for n in range(1, nz):
        link.send(v.m3.at[z], v.m3.at[z], d.s8.at[n], d.r8.at[n], place.zn(n))
    for n in range(1, nz):
        link.arrived(v.m3.at[(z - n + nz) % nz], d.s8.at[0], d.r8.at[n])
    max_out[...] = cap_value * jnp.tanh(jnp.max(v.m3[...], axis=0) / cap_value)
    link.finish()


class Named:
    pass


def whole_call(nz, *args):
    tok, _, pos, _, _, freq, wq, wk, wv, wo, q_gain, _, _, _, embed = args
    rows, model = tok.shape
    pack, width = pos.shape[1], q_gain.shape[1]
    grp = nz * NY
    count = grp * SEGS
    ring = lambda: [DMA((nz,)), DMA((nz,)), DMA((3, nz)), DMA((3, nz)), DMA((nz,)), DMA((nz,))]
    plain = lambda: [DMA((nz,)), DMA((nz,)), DMA((3,)), DMA((3,)), DMA((nz,)), DMA((nz,))]
    buffers = dict(
        emb=(embed.shape, BF16),
        tok_all=((NS, rows, model), BF16),
        w_all=((grp, wq.shape[0], 3 * width), BF16),
        wo_all=((NX, 2, grp) + wo.shape, BF16),
        pos_col=((pack, 128), F32),
        start_col=((pack, 128), F32),
        cos=((pack, 128), F32),
        sin=((pack, 128), F32),
        query=((pack, width), BF16),
        kv=((pack, 2 * width), BF16),
        att=((NS, rows, width), BF16),
        att_in=((NS, rows, width), BF16),
        kv_out=((rows, 2 * width), BF16),
        kv_in=((rows, 2 * width), BF16),
        summed=((rows, model), F32),
        st=((NS, SEGS, width), F32),
        own=((NS, SEGS, width), F32),
        zbuf=((nz, SEGS, width), F32),
        rows=((nz * SEGS, width), F32),
        buf=((NS, NY, nz * SEGS, width), BF16),
        m1=((NS, 1, count), F32),
        m2=((NY, 1, count), F32),
        m3=((nz, 1, count), F32),
    )
    pair = lambda a, b, shape: {a: DMA(shape), b: DMA(shape)}
    sems = dict(fetch=DMA, ts=DMA((7, CHUNKS)), tr=DMA((NS, CHUNKS)), ks=DMA, kr=DMA)
    sems |= pair("xs", "xr", (3,)) | pair("asend", "arecv", (4, 2))
    sems |= pair("s1", "r1", (NS,)) | pair("s2", "r2", (nz,)) | pair("s3", "r3", (NY,))
    sems |= pair("s4", "r4", (NX,)) | pair("s5", "r5", (NX,)) | pair("s6", "r6", (NS,))
    sems |= pair("s7", "r7", (NY,)) | pair("s8", "r8", (nz,))
    flows = [ring(), plain(), plain(), ring(), ring()]
    scratch = (
        [pltpu.VMEM(*b) for b in buffers.values()]
        + list(sems.values())
        + [sem for one in flows for sem in one]
    )

    def kernel(*refs):
        refs, extra = list(refs[:19]), list(refs[19:])
        v, d = Named(), Named()
        for name in buffers:
            setattr(v, name, extra.pop(0))
        for name in sems:
            setattr(d, name, extra.pop(0))
        groups = [tuple(extra[6 * n : 6 * n + 6]) for n in range(len(flows))]
        d.w, d.wo = groups[0], groups[1:]
        whole_kernel(nz, *refs, v, d)

    return pl.pallas_call(
        kernel,
        out_shape=(
            jax.ShapeDtypeStruct((rows, model), BF16),
            jax.ShapeDtypeStruct((rows, 2 * KEY_HEADS * width), BF16),
            jax.ShapeDtypeStruct((count, 1), F32),
            jax.ShapeDtypeStruct((1, count), F32),
        ),
        in_specs=[VMEM] * 14 + [ANY],
        out_specs=[VMEM] * 4,
        scratch_shapes=scratch,
        compiler_params=pltpu.CompilerParams(
            collective_id=0, has_side_effects=True, vmem_limit_bytes=56 * 1024 * 1024
        ),
        name="whole",
    )(*args)


def shards(
    tokens, seg_ids, deal, page_table, in_gain, w_query, key_weight, value_weight,
    q_gain, key_gain, w_out, post_gain, final_gain, embed,
):
    nz = lax.axis_size("grp") // NY
    half = q_gain.shape[0] // 2
    frequency = rope_base ** (-2.0 * jnp.arange(half, dtype=F32) / q_gain.shape[0])
    hidden, cache, norm, top = whole_call(
        nz, tokens[0], seg_ids, deal, page_table, in_gain[None], frequency[None],
        w_query, key_weight, value_weight, w_out.T, q_gain[None], key_gain[None],
        post_gain[None], final_gain[None], embed,
    )
    pages = cache.shape[0] // PAGE_SLOTS
    cache = cache.reshape(pages, PAGE_SLOTS, cache.shape[1])
    order = lambda v: v.reshape(NY, nz, SEGS).transpose(1, 0, 2).reshape(-1)
    return (hidden[None], cache[None], order(norm), order(top))


def solution(mesh):
    return jax.shard_map(
        shards,
        mesh=mesh,
        in_specs=(
            P("grp", "seq", None),
            P("grp", None),
            P("grp", None),
            P("grp", None),
            P(),
            P("grp", "seq"),
            P("grp", None),
            P("grp", None),
            P(),
            P(),
            P("seq", "grp"),
            P(),
            P(),
            P(("grp", "seq"), None),
        ),
        out_specs=(P("grp", "seq", None), P("grp", "seq", None, None), P(), P()),
        check_vma=False,
    )
```

time: 186 us -> 168 us (0.903)
  matrix products: 24.7 us -> 0 us
  Pallas kernels: 145 us -> 158 us
  other arithmetic: 11.8 us -> 2.82 us
  local copies, waits for them, and re-layouts: 2.87 us -> 5.66 us
    dot_general x13 -> x0, matrix products: 24.7 us -> none  [the longest x8 14.1 us: shards(): lax.dot_general(att_in[n], wo[n], (((1,), (1,)), ((), ())), preferred_ele...]
    pallas_call x3 -> x1, Pallas kernels: 145 us -> 158 us  [whole_call(): pl.pallas_call(kernel, out_shape=(jax.ShapeDtypeStruct((rows, model), BF1...]
    reduce_sum x5 -> x0, other arithmetic: 3.61 us -> none  [the longest x2 1.57 us: rows_scaled(): mean_square = jnp.mean(value_rows * value_rows, axis=-1, keepdims=True)]
    unnamed x24 -> x2, local copies, waits for them, and re-layouts: 0.07 us -> 3.55 us
    another operation x2 -> x0, other arithmetic: 3.2 us -> none
    convert_element_type x2 -> x0, other arithmetic: 2.27 us -> none  [the longest x1 2.03 us: shards(): normed = rows_scaled(own_tokens.astype(F32), in_gain).astype(BF16)]
where the time goes in v2:
time: 168 us; the launch traced here: 167 us
  Pallas kernels  158 us (94%)
  local copies, waits for them, and re-layouts  5.66 us (3%)
  other arithmetic  2.82 us (2%)
    pallas_call x1, Pallas kernels, whole_call(): pl.pallas_call(kernel, out_shape=(jax.ShapeDtypeStruct((rows, model), BF1...  158 us
    unnamed x2, local copies, waits for them, and re-layouts  3.55 us

profile of v2, /device:TPU:1, one launch (start us, length us, event | category | flops | bytes accessed | tf_op | source)
XLA Modules:
  0.0 167.3 jit_solution(6231617978367516126)
XLA Ops:
  0.6 0.5 multiply_power_fusion.refs_5_
  1.2 158.1 %whole.1 = (bf16[128,2048]{1,0:T(8,128)(2,1)}, bf16[128,1024]{1,0:T(8,128)(2,1)}, f32[256,1]{1,0:T(8,128)}, f32[1,256]{1,0:T(1,128)}) custom-call(bf16[128,2048]{1,0:T(8,128)(2,1)} %bitcast.12, s32[1,1024]{1,0:T(1,128)} %refs_1_.1, s32[1,1024]{1,0:T(1,128)} %refs_2_.1, s32[1,128]{1,0:T(1,128)} %refs_3_.1, f32[1,2048]{1,0:T(1,128)} %bitcast.17, ...), custom_call_target="tpu_custom_call" | custom-call | tf_op jit(solution)/shard_map/whole/pallas_call | solution.py:518
  159.3 0.5 broadcast.21
  159.8 1.3 reduce.4
  161.1 0.1 reshape.32
  161.2 0.7 reshape.33
  161.9 1.0 reduce
  162.9 0.1 reshape.30
  163.1 0.7 reshape.31
  163.8 1.9 %copy.22 = bf16[1,128,2048]{2,1,0:T(8,128)(2,1)} copy(bf16[1,128,2048]{2,1,0:T(8,128)(2,1)} %bitcast.11) | data formatting | bytes 1048576
  165.6 1.7 copy.23
  (2 shorter events, 0.0 us)

commit v3 on v2

--- a/solution.py
+++ b/solution.py
@@ -128,6 +128,7 @@
     zs, zr, ys, yr, ss, sr = sems
     half = place.nz // 2
     gy = lambda z, d: z * NY + (place.y + d + NY) % NY
+    direct = [q for k in (half - 1, half) for q, _, _ in slots(place, k)]
     for k in range(half + 3):
         for q, z, way in slots(place, k):
             here = block(gy(z, 0))
@@ -143,13 +144,18 @@
                 link.send(here, here, zs.at[q + 1], zr.at[q + 1], place.zn(-1))
             link.send(here, here, ys.at[0, q], yr.at[0, q], place.yn(1))
             link.send(here, here, ys.at[1, q], yr.at[1, q], place.yn(-1))
-        for q, z, way in slots(place, k - 1) if k >= 1 else []:
+            if k >= half - 1:
+                link.send(here, here, ys.at[2, q], yr.at[2, q], place.yn(2))
+        for q, z, way in slots(place, k - 2) if 2 <= k <= half else []:
             near = block(gy(z, -way))
             kind = 0 if way == 1 else 1
             link.arrived(near, zs.at[0], yr.at[kind, q])
             link.send(near, near, ys.at[2, q], yr.at[2, q], place.yn(way))
-        for q, z, way in slots(place, k - 2) if k >= 2 else []:
+        ready = [n for n in range(half + 1) if min(n + 4, half + 2) == k]
+        for q, z, way in [slot for n in ready for slot in slots(place, n)]:
             link.arrived(block(gy(z, way)), zs.at[0], yr.at[1 if way == 1 else 0, q])
+            if q in direct:
+                link.arrived(block(gy(z, -way)), zs.at[0], yr.at[0 if way == 1 else 1, q])
             link.arrived(block(gy(z, 2)), zs.at[0], yr.at[2, q])
             link.send(plane(z), plane(z), ss.at[q], sr.at[q], place.sib)
         yield
@@ -246,7 +252,7 @@
     peers = (
         [place.sn(n) for n in range(1, NS)]
         + [place.yn(n) for n in range(1, NY)]
-        + [place.zn(n) for n in range(1, nz)]
+        + [place.zn(1), place.zn(-1)]
     )
     entry = pltpu.get_barrier_semaphore()
     for peer in peers:
@@ -282,22 +288,26 @@
     def flow(n, way):
         return way(place, link, wo_block(n), wo_plane(n, c), wo_plane(n, 1 - c), d.wo[n])
 
-    first = together([
-        gather_zy(place, link, block, plane(c), plane(1 - c), d.w),
-        gather_rows(place, link, v.tok_all, d.ts, d.tr),
+    weights = gather_zy(place, link, block, plane(c), plane(1 - c), d.w)
+    tokens = gather_rows(place, link, v.tok_all, d.ts, d.tr)
+    background = together([
+        flow(0, gather_yz), flow(1, gather_yz), flow(2, gather_zy), flow(3, gather_zy)
     ])
-    next(first)
     own = v.wo_all.at[x, c, g]
-    for n, way in enumerate((1, -1, 2)):
-        link.send(own, own, d.xs.at[n], d.xr.at[n], place.xn(way))
-    next(first)
-    for n, way in enumerate((1, -1, 2)):
-        link.arrived(v.wo_all.at[(x - way + NX) % NX, c, g], d.xs.at[0], d.xr.at[n])
-    early = flow(0, gather_yz)
-    for _ in first:
-        pump(early, 1)
-    late = together([flow(1, gather_yz), flow(2, gather_zy), flow(3, gather_zy)])
-    background = together([early, late])
+    for t in range(nz // 2 + 4):
+        pump(weights, 1)
+        if t in (0, 3, 4, 5, 6) or t >= 7:
+            pump(tokens, 1)
+        if t == 0:
+            for n, way in enumerate((1, -1, 2)):
+                link.send(own, own, d.xs.at[n], d.xr.at[n], place.xn(way))
+        if t == 1:
+            for n, way in enumerate((1, -1, 2)):
+                link.arrived(v.wo_all.at[(x - way + NX) % NX, c, g], d.xs.at[0], d.xr.at[n])
+        if t >= 2:
+            pump(background, 1)
+    for _ in together([weights, tokens]):
+        pass
 
     pump(background, 1)
     rest = v.w_all[...].reshape(model, 3 * width)
@@ -337,7 +347,7 @@
             link.send(
                 v.att.at[there], v.att_in.at[s], d.asend.at[n, 1], d.arecv.at[n, 1], {"seq": there}
             )
-        pump(background, 2)
+        pump(background, 1)
 
     table = column(pages[...].astype(F32))
     whole, within = pos[...] // PAGE_SLOTS, pos[...] % PAGE_SLOTS
@@ -427,7 +437,7 @@
         value = v.buf[n].reshape(count, width).astype(F32)
         total = total + jnp.sum(value * value, axis=1, keepdims=True)
     mean = total / model
-    norm_out[...] = jnp.sqrt(mean)
+    norm_row = jnp.broadcast_to(jnp.sqrt(mean), (count, 128)).T[:8]
     scale = lax.rsqrt(mean + eps)
     fetch.wait()
     logits = jnp.zeros((v.emb.shape[0], count), F32)
@@ -450,7 +460,21 @@
         link.send(v.m3.at[z], v.m3.at[z], d.s8.at[n], d.r8.at[n], place.zn(n))
     for n in range(1, nz):
         link.arrived(v.m3.at[(z - n + nz) % nz], d.s8.at[0], d.r8.at[n])
-    max_out[...] = cap_value * jnp.tanh(jnp.max(v.m3[...], axis=0) / cap_value)
+    top = cap_value * jnp.tanh(jnp.max(v.m3[...], axis=0) / cap_value)
+    both = jnp.where(lax.broadcasted_iota(jnp.int32, (8, count), 0) == 0, top, norm_row)
+    line = lax.broadcasted_iota(jnp.int32, (count, count), 0)
+    place_of = lax.broadcasted_iota(jnp.int32, (count, count), 1)
+    line_of = (
+        place_of // SEGS % NY * (nz * SEGS) + place_of // (NY * SEGS) * SEGS + place_of % SEGS
+    )
+    both = jnp.dot(
+        both,
+        (line == line_of).astype(F32),
+        precision=lax.Precision.HIGHEST,
+        preferred_element_type=F32,
+    )
+    max_out[...] = both[0:1]
+    norm_out[...] = both[1:2]
     link.finish()
 
 
@@ -520,7 +544,7 @@
         out_shape=(
             jax.ShapeDtypeStruct((rows, model), BF16),
             jax.ShapeDtypeStruct((rows, 2 * KEY_HEADS * width), BF16),
-            jax.ShapeDtypeStruct((count, 1), F32),
+            jax.ShapeDtypeStruct((1, count), F32),
             jax.ShapeDtypeStruct((1, count), F32),
         ),
         in_specs=[VMEM] * 14 + [ANY],
@@ -531,6 +555,22 @@
         ),
         name="whole",
     )(*args)
+
+
+def store_kernel(*refs):
+    half = len(refs) // 2
+    for source, target in zip(refs[:half], refs[half:]):
+        target[...] = source[...]
+
+
+def store_call(*arrays):
+    return pl.pallas_call(
+        store_kernel,
+        out_shape=[jax.ShapeDtypeStruct(a.shape, a.dtype) for a in arrays],
+        in_specs=[VMEM] * len(arrays),
+        out_specs=[VMEM] * len(arrays),
+        name="store",
+    )(*arrays)
 
 
 def shards(
@@ -545,10 +585,10 @@
         w_query, key_weight, value_weight, w_out.T, q_gain[None], key_gain[None],
         post_gain[None], final_gain[None], embed,
     )
+    hidden, cache, norm, top = store_call(hidden, cache, norm, top)
     pages = cache.shape[0] // PAGE_SLOTS
     cache = cache.reshape(pages, PAGE_SLOTS, cache.shape[1])
-    order = lambda v: v.reshape(NY, nz, SEGS).transpose(1, 0, 2).reshape(-1)
-    return (hidden[None], cache[None], order(norm), order(top))
+    return (hidden[None], cache[None], norm[0], top[0])
 
 
 def solution(mesh):

time: 168 us -> 141 us (0.84)
  Pallas kernels: 158 us -> 139 us
  local copies, waits for them, and re-layouts: 5.66 us -> 0 us
  other arithmetic: 2.82 us -> 0.53 us
    pallas_call x1, Pallas kernels: 158 us -> 137 us  [whole_call(): pl.pallas_call(kernel, out_shape=(jax.ShapeDtypeStruct((rows, model), BF1...]
    unnamed x2 -> x0, local copies, waits for them, and re-layouts: 3.55 us -> none
    pallas_call x2 -> x0, other arithmetic: 2.3 us -> none  [whole_call(): pl.pallas_call(kernel, out_shape=(jax.ShapeDtypeStruct((rows, model), BF1...]
    pallas_call x0 -> x1, Pallas kernels: none -> 2.03 us  [store_call(): pl.pallas_call(store_kernel, out_shape=[jax.ShapeDtypeStruct(a.shape, a.d...]
where the time goes in v3:
time: 141 us; the launch traced here: 140 us
  Pallas kernels  139 us (99%)
    pallas_call x1, Pallas kernels, whole_call(): pl.pallas_call(kernel, out_shape=(jax.ShapeDtypeStruct((rows, model), BF1...  137 us

profile of v3, /device:TPU:1, one launch (start us, length us, event | category | flops | bytes accessed | tf_op | source)
XLA Modules:
  0.0 140.4 jit_solution(12361648655008741074)
XLA Ops:
  0.6 0.5 multiply_power_fusion.refs_5_
  1.2 137.2 %whole.1 = (bf16[128,2048]{1,0:T(8,128)(2,1)}, bf16[128,1024]{1,0:T(8,128)(2,1)}, f32[1,256]{1,0:T(1,128)}, f32[1,256]{1,0:T(1,128)}) custom-call(bf16[128,2048]{1,0:T(8,128)(2,1)} %bitcast.11, s32[1,1024]{1,0:T(1,128)} %refs_1_.1, s32[1,1024]{1,0:T(1,128)} %refs_2_.1, s32[1,128]{1,0:T(1,128)} %refs_3_.1, f32[1,2048]{1,0:T(1,128)} %bitcast.13, ...), custom_call_target="tpu_custom_call" | custom-call | tf_op jit(solution)/shard_map/whole/pallas_call | solution.py:542
  138.4 2.0 %store.1 = (bf16[128,2048]{1,0:T(8,128)(2,1)}, bf16[128,1024]{1,0:T(8,128)(2,1)}, f32[1,256]{1,0:T(1,128)}, f32[1,256]{1,0:T(1,128)}) custom-call(bf16[128,2048]{1,0:T(8,128)(2,1)} %get-tuple-element.12.refs_0_, bf16[128,1024]{1,0:T(8,128)(2,1)} %get-tuple-element.13.refs_1_, f32[1,256]{1,0:T(1,128)} %get-tuple-element.14.refs_2_, ...), custom_call_target="tpu_custom_call" | custom-call | tf_op jit(solution)/shard_map/store/pallas_call | solution.py:567

commit v4 on v3

--- a/solution.py
+++ b/solution.py
@@ -271,12 +271,25 @@
     start = jnp.zeros_like(position)
     for end in ends[:-1]:
         start = jnp.maximum(start, jnp.where(position >= end, end, 0.0))
-    for n in range(pack // 128):
-        block = slice(n * 128, (n + 1) * 128)
-        pos_col, start_col = column(position[:, block]), column(start[:, block])
-        v.pos_col[block], v.start_col[block] = pos_col, start_col
-        angle = (pos_col - start_col) * freq[...]
-        v.cos[block], v.sin[block] = jnp.cos(angle), jnp.sin(angle)
+    v.la[...] = jnp.zeros_like(v.la)
+
+    def bounds(size):
+        line = lax.broadcasted_iota(jnp.int32, (16, size), 0)
+        first, last = jnp.zeros((16, size), F32), jnp.full((16, size), -1.0, F32)
+        for j in range(SEGS):
+            last = jnp.where(line == j, ends[j] - 1.0, last)
+            if j > 0:
+                first = jnp.where(line == j, ends[j - 1], first)
+        return first, last
+
+    def rope_tables():
+        for n in range(pack // 128):
+            block = slice(n * 128, (n + 1) * 128)
+            pos_col, start_col = column(position[:, block]), column(start[:, block])
+            v.pos_col[block], v.start_col[block] = pos_col, start_col
+            angle = (pos_col - start_col) * freq[...]
+            v.cos[block], v.sin[block] = jnp.cos(angle), jnp.sin(angle)
+            yield
 
     pl.semaphore_wait(entry, len(peers))
 
@@ -293,6 +306,7 @@
     background = together([
         flow(0, gather_yz), flow(1, gather_yz), flow(2, gather_zy), flow(3, gather_zy)
     ])
+    tables = rope_tables()
     own = v.wo_all.at[x, c, g]
     for t in range(nz // 2 + 4):
         pump(weights, 1)
@@ -301,12 +315,22 @@
         if t == 0:
             for n, way in enumerate((1, -1, 2)):
                 link.send(own, own, d.xs.at[n], d.xr.at[n], place.xn(way))
+            _, last = bounds(rows)
+            select = (last == pos[:, lanes(s * rows, rows)].astype(F32)).astype(BF16)
+            found = jnp.dot(select, tok[...], preferred_element_type=F32).astype(BF16)
+            for n in range(NS):
+                v.tl_out[n] = found[:, n * width : (n + 1) * width]
+            v.tl_in[s] = v.tl_out[s]
+            for n in range(1, NS):
+                to = (s + n) % NS
+                link.send(v.tl_out.at[to], v.tl_in.at[s], d.s1.at[n], d.r1.at[n], {"seq": to})
         if t == 1:
             for n, way in enumerate((1, -1, 2)):
                 link.arrived(v.wo_all.at[(x - way + NX) % NX, c, g], d.xs.at[0], d.xr.at[n])
         if t >= 2:
             pump(background, 1)
-    for _ in together([weights, tokens]):
+        pump(tables, 1)
+    for _ in together([weights, tokens, tables]):
         pass
 
     pump(background, 1)
@@ -326,6 +350,49 @@
         v.kv[here, :width] = key.astype(BF16)
         v.kv[here, width:] = scaled(raw[:, 2 * width :], None).astype(BF16)
         pump(background, 1)
+
+    first, last = bounds(pack)
+    select = (last == position).astype(BF16)
+    query = jnp.dot(select, v.query[...], preferred_element_type=F32).astype(BF16)
+    masked = jnp.where(
+        (position <= last) & (position >= first), nt(query, v.kv[:, :width]), -1e30
+    )
+    raw = jnp.exp(masked - jnp.max(masked, axis=1, keepdims=True))
+    weights = (raw / jnp.sum(raw, axis=1, keepdims=True)).astype(BF16)
+    attended = jnp.dot(weights, v.kv[:, width:], preferred_element_type=F32)
+    v.la[s, 0:16] = attended.astype(BF16)
+    mine = v.la.at[s, pl.ds(0, 16)]
+    for n in range(1, NS):
+        link.send(mine, mine, d.ls.at[n], d.lr.at[n], place.sn(n))
+    for _ in background:
+        pass
+    for n in range(1, NS):
+        link.arrived(v.la.at[(s - n + NS) % NS, pl.ds(0, 16)], d.ls.at[0], d.lr.at[n])
+        link.arrived(v.tl_in.at[(s - n + NS) % NS], d.s1.at[0], d.r1.at[n])
+
+    span = 512
+    depth = wo.shape[0]
+
+    def project(source):
+        for m in range(model // span):
+            total = jnp.zeros((span, rows), F32)
+            for n in range(NS):
+                w = v.wo_all[n // 2, n % 2, m * span // depth : (m + 1) * span // depth]
+                total = total + nt(w.reshape(span, width), source[n]).astype(BF16).astype(F32)
+            for n in range(span // 128):
+                v.summed[:, m * span + n * 128 : m * span + (n + 1) * 128] = total[
+                    n * 128 : (n + 1) * 128
+                ].T
+
+    project(v.la)
+    total = v.summed[0:16]
+    scale = lax.rsqrt(jnp.mean(total * total, axis=1, keepdims=True) + eps)
+    here = lanes(s * width, width)
+    total = v.summed[0:16, here] * scale * post_gain[:, here]
+    states = (jnp.sum(v.tl_in[...].astype(F32), axis=0) + total).astype(BF16).astype(F32)
+    v.zbuf[z] = states[:SEGS]
+    for n in range(1, nz):
+        link.send(v.zbuf.at[z], v.zbuf.at[z], d.s2.at[n], d.r2.at[n], place.zn(n))
 
     for n, way in enumerate((2, 1, -1, 0)):
         chip = (x + way + NX) % NX
@@ -347,7 +414,14 @@
             link.send(
                 v.att.at[there], v.att_in.at[s], d.asend.at[n, 1], d.arecv.at[n, 1], {"seq": there}
             )
-        pump(background, 1)
+
+    for n in range(1, nz):
+        link.arrived(v.zbuf.at[(z - n + nz) % nz], d.s2.at[0], d.r2.at[n])
+    for n in range(nz):
+        v.rows[n * SEGS : (n + 1) * SEGS] = v.zbuf[n]
+    v.buf[s, y] = v.rows[...].astype(BF16)
+    for n in range(1, NY):
+        link.send(v.buf.at[s, y], v.buf.at[s, y], d.s3.at[n], d.r3.at[n], place.yn(n))
 
     table = column(pages[...].astype(F32))
     whole, within = pos[...] // PAGE_SLOTS, pos[...] % PAGE_SLOTS
@@ -363,67 +437,30 @@
         if n == 0:
             v.kv_out[...] = picked
             link.send(v.kv_out, v.kv_in, d.ks, d.kr, {"seq": partner})
-            pump(background, 1)
         else:
             mine = x // 2 * width
             cache_out[:, lanes(mine, width)] = picked[:, :width]
             cache_out[:, lanes(KEY_HEADS * width + mine, width)] = picked[:, width:]
-    for _ in background:
-        pass
+
+    for n in range(1, NY):
+        link.arrived(v.buf.at[s, (y - n + NY) % NY], d.s3.at[0], d.r3.at[n])
+    for n in range(1, NX):
+        link.send(v.buf.at[s], v.buf.at[s], d.s4.at[n], d.r4.at[n], place.xn(n))
+    link.send(v.buf.at[s], v.buf.at[s], d.s4.at[0], d.r4.at[0], place.sib)
+
     for n, way in enumerate((2, 1, -1, 0)):
         chip = (x - way + NX) % NX
         link.arrived(v.att_in.at[2 * chip + 1 - c], d.asend.at[0, 0], d.arecv.at[n, 0])
         if way != 0:
             link.arrived(v.att_in.at[2 * chip + c], d.asend.at[0, 0], d.arecv.at[n, 1])
-
-    span = 512
-    depth = wo.shape[0]
-    for m in range(model // span):
-        total = jnp.zeros((span, rows), F32)
-        for n in range(NS):
-            w = v.wo_all[n // 2, n % 2, m * span // depth : (m + 1) * span // depth]
-            total = total + nt(w.reshape(span, width), v.att_in[n]).astype(BF16).astype(F32)
-        for n in range(span // 128):
-            v.summed[:, m * span + n * 128 : m * span + (n + 1) * 128] = total[
-                n * 128 : (n + 1) * 128
-            ].T
-    hidden = (tok[...].astype(F32) + scaled(v.summed[...], post_gain[...])).astype(BF16)
-    hidden_out[...] = hidden
-
-    own_pos = pos[:, lanes(s * rows, rows)].astype(F32)
-    line = lax.broadcasted_iota(jnp.int32, (16, rows), 0)
-    last = jnp.full((16, rows), -1.0, F32)
-    for j in range(SEGS):
-        last = jnp.where(line == j, ends[j] - 1.0, last)
-    select = (last == own_pos).astype(BF16)
-    states = jnp.dot(select, hidden, preferred_element_type=F32)
-    for n in range(NS):
-        v.st[n] = states[:SEGS, n * width : (n + 1) * width]
-    v.own[s] = v.st[s]
-    for n in range(1, NS):
-        to = (s + n) % NS
-        link.send(v.st.at[to], v.own.at[s], d.s1.at[n], d.r1.at[n], {"seq": to})
+    project(v.att_in)
+    hidden = tok[...].astype(F32) + scaled(v.summed[...], post_gain[...])
+    hidden_out[...] = hidden.astype(BF16)
     link.arrived(v.kv_in, d.ks, d.kr)
     other = (1 - x // 2) * width
     cache_out[:, lanes(other, width)] = v.kv_in[:, :width]
     cache_out[:, lanes(KEY_HEADS * width + other, width)] = v.kv_in[:, width:]
-    for n in range(1, NS):
-        link.arrived(v.own.at[(s - n + NS) % NS], d.s1.at[0], d.r1.at[n])
-    v.zbuf[z] = jnp.sum(v.own[...], axis=0)
-    for n in range(1, nz):
-        link.send(v.zbuf.at[z], v.zbuf.at[z], d.s2.at[n], d.r2.at[n], place.zn(n))
-    for n in range(1, nz):
-        link.arrived(v.zbuf.at[(z - n + nz) % nz], d.s2.at[0], d.r2.at[n])
-    for n in range(nz):
-        v.rows[n * SEGS : (n + 1) * SEGS] = v.zbuf[n]
-    v.buf[s, y] = v.rows[...].astype(BF16)
-    for n in range(1, NY):
-        link.send(v.buf.at[s, y], v.buf.at[s, y], d.s3.at[n], d.r3.at[n], place.yn(n))
-    for n in range(1, NY):
-        link.arrived(v.buf.at[s, (y - n + NY) % NY], d.s3.at[0], d.r3.at[n])
-    for n in range(1, NX):
-        link.send(v.buf.at[s], v.buf.at[s], d.s4.at[n], d.r4.at[n], place.xn(n))
-    link.send(v.buf.at[s], v.buf.at[s], d.s4.at[0], d.r4.at[0], place.sib)
+
     for n in (1, 3, 2):
         came = v.buf.at[place.xs(-n)]
         link.arrived(came, d.s4.at[0], d.r4.at[n])
@@ -445,17 +482,15 @@
         value = v.buf[n].reshape(count, width).astype(F32)
         final = (value * scale * final_gain[:, n * width : (n + 1) * width]).astype(BF16)
         logits = logits + nt(v.emb[:, n * width : (n + 1) * width], final)
-    v.m1[s] = jnp.max(logits, axis=0, keepdims=True)
-    for n in range(1, NS):
-        link.send(v.m1.at[s], v.m1.at[s], d.s6.at[n], d.r6.at[n], place.sn(n))
-    for n in range(1, NS):
-        link.arrived(v.m1.at[(s - n + NS) % NS], d.s6.at[0], d.r6.at[n])
-    v.m2[y] = jnp.max(v.m1[...], axis=0)
-    for n in range(1, NY):
-        link.send(v.m2.at[y], v.m2.at[y], d.s7.at[n], d.r7.at[n], place.yn(n))
-    for n in range(1, NY):
-        link.arrived(v.m2.at[(y - n + NY) % NY], d.s7.at[0], d.r7.at[n])
-    v.m3[z] = jnp.max(v.m2[...], axis=0)
+    near = [(a, b) for a in range(NY) for b in range(NS)]
+    v.m1[y * NS + s] = jnp.max(logits, axis=0, keepdims=True)
+    for n, (a, b) in enumerate(near[1:], 1):
+        to = {"grp": z * NY + (y + a) % NY, "seq": (s + b) % NS}
+        link.send(v.m1.at[y * NS + s], v.m1.at[y * NS + s], d.s6.at[n], d.r6.at[n], to)
+    for n, (a, b) in enumerate(near[1:], 1):
+        slot = (y - a + NY) % NY * NS + (s - b + NS) % NS
+        link.arrived(v.m1.at[slot], d.s6.at[0], d.r6.at[n])
+    v.m3[z] = jnp.max(v.m1[...], axis=0)
     for n in range(1, nz):
         link.send(v.m3.at[z], v.m3.at[z], d.s8.at[n], d.r8.at[n], place.zn(n))
     for n in range(1, nz):
@@ -506,21 +541,21 @@
         kv_out=((rows, 2 * width), BF16),
         kv_in=((rows, 2 * width), BF16),
         summed=((rows, model), F32),
-        st=((NS, SEGS, width), F32),
-        own=((NS, SEGS, width), F32),
+        la=((NS, rows, width), BF16),
+        tl_out=((NS, 16, width), BF16),
+        tl_in=((NS, 16, width), BF16),
         zbuf=((nz, SEGS, width), F32),
         rows=((nz * SEGS, width), F32),
         buf=((NS, NY, nz * SEGS, width), BF16),
-        m1=((NS, 1, count), F32),
-        m2=((NY, 1, count), F32),
+        m1=((NY * NS, 1, count), F32),
         m3=((nz, 1, count), F32),
     )
     pair = lambda a, b, shape: {a: DMA(shape), b: DMA(shape)}
     sems = dict(fetch=DMA, ts=DMA((7, CHUNKS)), tr=DMA((NS, CHUNKS)), ks=DMA, kr=DMA)
     sems |= pair("xs", "xr", (3,)) | pair("asend", "arecv", (4, 2))
     sems |= pair("s1", "r1", (NS,)) | pair("s2", "r2", (nz,)) | pair("s3", "r3", (NY,))
-    sems |= pair("s4", "r4", (NX,)) | pair("s5", "r5", (NX,)) | pair("s6", "r6", (NS,))
-    sems |= pair("s7", "r7", (NY,)) | pair("s8", "r8", (nz,))
+    sems |= pair("s4", "r4", (NX,)) | pair("s5", "r5", (NX,)) | pair("s6", "r6", (NY * NS,))
+    sems |= pair("ls", "lr", (NS,)) | pair("s8", "r8", (nz,))
     flows = [ring(), plain(), plain(), ring(), ring()]
     scratch = (
         [pltpu.VMEM(*b) for b in buffers.values()]

time: 141 us -> 132 us (0.936)
  Pallas kernels: 139 us -> 130 us
    pallas_call x1, Pallas kernels: 137 us -> 128 us  [whole_call(): pl.pallas_call(kernel, out_shape=(jax.ShapeDtypeStruct((rows, model), BF1...]
where the time goes in v4:
time: 132 us
  Pallas kernels  130 us (98%)
    pallas_call x1, Pallas kernels, whole_call(): pl.pallas_call(kernel, out_shape=(jax.ShapeDtypeStruct((rows, model), BF1...  128 us

profile of v4, /device:TPU:1, one launch (start us, length us, event | category | flops | bytes accessed | tf_op | source)
XLA Modules:
  0.0 131.6 jit_solution(13608815015047223535)
XLA Ops:
  0.6 0.5 multiply_power_fusion.refs_5_
  1.2 128.4 %whole.1 = (bf16[128,2048]{1,0:T(8,128)(2,1)}, bf16[128,1024]{1,0:T(8,128)(2,1)}, f32[1,256]{1,0:T(1,128)}, f32[1,256]{1,0:T(1,128)}) custom-call(bf16[128,2048]{1,0:T(8,128)(2,1)} %bitcast.11, s32[1,1024]{1,0:T(1,128)} %refs_1_.1, s32[1,1024]{1,0:T(1,128)} %refs_2_.1, s32[1,128]{1,0:T(1,128)} %refs_3_.1, f32[1,2048]{1,0:T(1,128)} %bitcast.13, ...), custom_call_target="tpu_custom_call" | custom-call | tf_op jit(solution)/shard_map/whole/pallas_call | solution.py:577
  129.5 2.0 %store.1 = (bf16[128,2048]{1,0:T(8,128)(2,1)}, bf16[128,1024]{1,0:T(8,128)(2,1)}, f32[1,256]{1,0:T(1,128)}, f32[1,256]{1,0:T(1,128)}) custom-call(bf16[128,2048]{1,0:T(8,128)(2,1)} %get-tuple-element.12.refs_0_, bf16[128,1024]{1,0:T(8,128)(2,1)} %get-tuple-element.13.refs_1_, f32[1,256]{1,0:T(1,128)} %get-tuple-element.14.refs_2_, ...), custom_call_target="tpu_custom_call" | custom-call | tf_op jit(solution)/shard_map/store/pallas_call | solution.py:602

commit v5 on v4

--- a/solution.py
+++ b/solution.py
@@ -304,17 +304,17 @@
     weights = gather_zy(place, link, block, plane(c), plane(1 - c), d.w)
     tokens = gather_rows(place, link, v.tok_all, d.ts, d.tr)
     background = together([
-        flow(0, gather_yz), flow(1, gather_yz), flow(2, gather_zy), flow(3, gather_zy)
+        flow(2, gather_zy), flow(3, gather_zy), flow(0, gather_yz), flow(1, gather_yz)
     ])
     tables = rope_tables()
     own = v.wo_all.at[x, c, g]
+    for n, way in enumerate((1, -1, 2)):
+        link.send(own, own, d.xs.at[n], d.xr.at[n], place.xn(way))
     for t in range(nz // 2 + 4):
         pump(weights, 1)
         if t in (0, 3, 4, 5, 6) or t >= 7:
             pump(tokens, 1)
         if t == 0:
-            for n, way in enumerate((1, -1, 2)):
-                link.send(own, own, d.xs.at[n], d.xr.at[n], place.xn(way))
             _, last = bounds(rows)
             select = (last == pos[:, lanes(s * rows, rows)].astype(F32)).astype(BF16)
             found = jnp.dot(select, tok[...], preferred_element_type=F32).astype(BF16)
@@ -327,7 +327,7 @@
         if t == 1:
             for n, way in enumerate((1, -1, 2)):
                 link.arrived(v.wo_all.at[(x - way + NX) % NX, c, g], d.xs.at[0], d.xr.at[n])
-        if t >= 2:
+        if t >= 1:
             pump(background, 1)
         pump(tables, 1)
     for _ in together([weights, tokens, tables]):

time: 132 us -> 120 us (0.909)
  Pallas kernels: 130 us -> 118 us
    pallas_call x1, Pallas kernels: 128 us -> 116 us  [whole_call(): pl.pallas_call(kernel, out_shape=(jax.ShapeDtypeStruct((rows, model), BF1...]
where the time goes in v5:
time: 120 us; the launch traced here: 119 us
  Pallas kernels  118 us (98%)
    pallas_call x1, Pallas kernels, whole_call(): pl.pallas_call(kernel, out_shape=(jax.ShapeDtypeStruct((rows, model), BF1...  116 us

profile of v5, /device:TPU:1, one launch (start us, length us, event | category | flops | bytes accessed | tf_op | source)
XLA Modules:
  0.0 119.4 jit_solution(227804569567772934)
XLA Ops:
  0.6 0.5 multiply_power_fusion.refs_5_
  1.2 116.2 %whole.1 = (bf16[128,2048]{1,0:T(8,128)(2,1)}, bf16[128,1024]{1,0:T(8,128)(2,1)}, f32[1,256]{1,0:T(1,128)}, f32[1,256]{1,0:T(1,128)}) custom-call(bf16[128,2048]{1,0:T(8,128)(2,1)} %bitcast.11, s32[1,1024]{1,0:T(1,128)} %refs_1_.1, s32[1,1024]{1,0:T(1,128)} %refs_2_.1, s32[1,128]{1,0:T(1,128)} %refs_3_.1, f32[1,2048]{1,0:T(1,128)} %bitcast.13, ...), custom_call_target="tpu_custom_call" | custom-call | tf_op jit(solution)/shard_map/whole/pallas_call | solution.py:577
  117.4 2.0 %store.1 = (bf16[128,2048]{1,0:T(8,128)(2,1)}, bf16[128,1024]{1,0:T(8,128)(2,1)}, f32[1,256]{1,0:T(1,128)}, f32[1,256]{1,0:T(1,128)}) custom-call(bf16[128,2048]{1,0:T(8,128)(2,1)} %get-tuple-element.12.refs_0_, bf16[128,1024]{1,0:T(8,128)(2,1)} %get-tuple-element.13.refs_1_, f32[1,256]{1,0:T(1,128)} %get-tuple-element.14.refs_2_, ...), custom_call_target="tpu_custom_call" | custom-call | tf_op jit(solution)/shard_map/store/pallas_call | solution.py:602
